TPU v7x, 32 devices: a whole 2x2x4 slice. The times are simulated.
32 devices in a mesh: win: 2 (over y), gz: 4 (over z), gy: 2 (over x), gx: 2 (over core).
Axes of the slice: x: 2, y: 2, z: 4, core: 2. Of those that a mesh axis runs over, the one named last changes fastest.
Arguments:
- noisy: float32 [32, 16, 256], P(('win', 'gz'), 'gy', 'gx'), parts along dimension 0, may hold values from -6 to 6
- first_weight: float32 [32, 1, 27], replicated, may hold values from -1.25 to 1.25
- first_bias: float32 [16], replicated, may hold values from -8 to -3
- second_weight: float32 [32, 16, 27], replicated, may hold values from -0.3125 to 0.3125
- second_bias: float32 [16], replicated, may hold values from -8 to -3
- head_weight: float32 [16], replicated, may hold values from -18 to 18
- seg_weight_in: float32 [16, 1, 27], replicated, may hold values from -1.25 to 1.25
- seg_bias_in: float32 [16], replicated, may hold values from -3 to 3
- seg_weight_out: float32 [16, 16, 27], replicated, may hold values from -0.3125 to 0.3125
- seg_bias_out: float32 [16], replicated, may hold values from -3 to 3
Outputs:
- denoised: float32 [32, 16, 256], P(('win', 'gz'), 'gy', 'gx'), parts along dimension 0
- segmented: float32 [16, 32, 16, 256], P(None, ('win', 'gz'), 'gy', 'gx'), parts along dimension 1
There are 2 independent parts, one for each index of `win`. A program takes and returns all parts, laid end to end along the dimension named above; an argument that names none is the same for every part. Nothing has to cross between parts.
All inputs are finite; a program needn't handle non-finite values.
Results may differ from a plain program's by a relative error of at most 0.00029.
Values sent between devices are 32-bit elements; how exact they have to be, the bound alone decides.
A program may use at most 64 MiB of HBM per device.

v0:
```python
import functools

import jax
import jax.numpy as jnp
from jax import lax
from jax.experimental import pallas as pl
from jax.experimental.pallas import tpu as pltpu
from jax.sharding import PartitionSpec as P

LANES = 128
F32 = jnp.float32
BF16 = jnp.bfloat16
MESH = pl.DeviceIdType.MESH


def split(value):
    high = value.astype(BF16)
    return high, (value - high.astype(F32)).astype(BF16)


def left_rows(weight):
    high, low = split(weight)
    return jnp.concatenate([high, high, low], axis=1)


def right_rows(high, low):
    return jnp.concatenate([high, low, high], axis=0)


def mxu(left, right):
    return jnp.dot(left, right, preferred_element_type=F32)


def lane_of(shape):
    return lax.broadcasted_iota(jnp.int32, shape, len(shape) - 1)


def row_of(shape):
    return lax.broadcasted_iota(jnp.int32, shape, 0)


def column(row_ref):
    count = row_ref.shape[1]
    shape = (count, count)
    spread = jnp.broadcast_to(row_ref[...], shape)
    return jnp.sum(jnp.where(row_of(shape) == lane_of(shape), spread, 0.0), axis=1, keepdims=True)


def times(count, step, carry, backward=False):
    if count <= 16:
        for i in range(count):
            carry = step(count - 1 - i if backward else i, carry)
        return carry
    return lax.fori_loop(0, count, lambda i, c: step(count - 1 - i if backward else i, c), carry)


def aligned(start, unit):
    return start if isinstance(start, int) else pl.multiple_of(start, unit)


def gather_kernel(sizes, by, noisy_ref, m1, x1, my, xy, where_ref, halo, m1_send, m1_recv, x1_send, x1_recv):
    gz, gy, gx = sizes
    me = lax.axis_index("gz")
    at_y = lax.axis_index("gy")
    at_x = lax.axis_index("gx")
    low_slab = me == 0
    high_slab = me == gz - 1

    def exists(dy, dx):
        ok = None
        for where, step, count in ((at_y, dy, gy), (at_x, dx, gx)):
            if step == 0:
                continue
            here = where > 0 if step < 0 else where < count - 1
            ok = here if ok is None else ok & here
        return ok

    def when(ok, action):
        if ok is None:
            action()
        else:
            pl.when(ok)(action)

    def device(z, dy, dx):
        return {
            "win": lax.axis_index("win"),
            "gz": z,
            "gy": lax.rem(at_y + dy + gy, gy),
            "gx": lax.rem(at_x + dx + gx, gx),
        }

    def peer(k):
        return lax.rem(me + k, gz)

    steps_y = (0,) + ((-1, 1) if gy > 1 else ())
    steps_x = (0,) + ((-1, 1) if gx > 1 else ())

    for side, first in ((0, 0), (1, by - 2)):
        for z in range(noisy_ref.shape[0] // by):
            halo[side, 2 * z : 2 * z + 2, :] = noisy_ref[z * by + first : z * by + first + 2, :]

    def payload(dy):
        return noisy_ref if dy == 0 else halo.at[(dy + 1) // 2]

    def slot(edge, dy, z):
        if dy == 0:
            return (x1 if edge else m1).at[z]
        return (xy if edge else my).at[(dy + 1) // 2, z]

    barrier = pltpu.get_barrier_semaphore()
    for dy in steps_y:
        for dx in steps_x:
            for k in range(gz):
                if (dy, dx, k) != (0, 0, 0):
                    def greet(dy=dy, dx=dx, k=k):
                        pl.semaphore_signal(
                            barrier, inc=1, device_id=device(peer(k), dy, dx), device_id_type=MESH
                        )
                    when(exists(dy, dx), greet)
    span_y = 1 + (at_y > 0).astype(jnp.int32) + (at_y < gy - 1).astype(jnp.int32)
    span_x = 1 + (at_x > 0).astype(jnp.int32) + (at_x < gx - 1).astype(jnp.int32)
    pl.semaphore_wait(barrier, gz * span_y * span_x - 1)

    def noisy_middle(dy, k):
        target = peer(k)
        return pltpu.make_async_remote_copy(
            src_ref=payload(dy),
            dst_ref=slot(False, -dy, me),
            send_sem=m1_send.at[dy + 1, k],
            recv_sem=m1_recv.at[1 - dy, me],
            device_id=device(target, dy, 0),
            device_id_type=MESH,
        )

    def noisy_edge(dy, dx):
        target = 0 if dx > 0 else gz - 1
        side = (dx + 1) // 2
        return pltpu.make_async_remote_copy(
            src_ref=payload(dy),
            dst_ref=slot(True, -dy, me),
            send_sem=x1_send.at[dy + 1, side],
            recv_sem=x1_recv.at[1 - dy, me],
            device_id=device(target, dy, dx),
            device_id_type=MESH,
        )

    sends = []
    for dy in steps_y:
        for k in range(gz - 1, -1, -1):
            if (dy, k) != (0, 0):
                sends.append((exists(dy, 0), functools.partial(noisy_middle, dy, k)))
    for dy in steps_y:
        for dx in steps_x:
            if dx != 0:
                sends.append((exists(dy, dx), functools.partial(noisy_edge, dy, dx)))
    for ok, make in sends:
        when(ok, lambda make=make: make().start())

    for i, value in enumerate((me, at_y, at_x)):
        where_ref[i] = value
    m1[me] = noisy_ref[...]
    for index, ok in ((0, at_y == 0), (1, at_y == gy - 1)):
        def no_row(index=index):
            for z in range(gz):
                my[index, z] = jnp.zeros(my.shape[2:], F32)
                xy[index, z] = jnp.zeros(xy.shape[2:], F32)
        pl.when(ok)(no_row)
    no_edge = jnp.logical_not((low_slab & (at_x > 0)) | (high_slab & (at_x < gx - 1)))

    def no_neighbour():
        x1[...] = jnp.zeros(x1.shape, F32)
        xy[...] = jnp.zeros(xy.shape, F32)

    pl.when(no_edge)(no_neighbour)
    for dy in steps_y:
        for k in range(gz):
            if (dy, k) != (0, 0):
                source = peer(k)
                def await_middle(dy=dy, source=source):
                    pltpu.make_async_remote_copy(
                        src_ref=payload(dy),
                        dst_ref=slot(False, dy, source),
                        send_sem=m1_send.at[1 + dy, 0],
                        recv_sem=m1_recv.at[1 + dy, source],
                        device_id=device(source, dy, 0),
                        device_id_type=MESH,
                    ).wait_recv()
                when(exists(dy, 0), await_middle)
    for dy in steps_y:
        for dx in steps_x:
            if dx != 0:
                ok = exists(dy, dx) & (low_slab if dx < 0 else high_slab)
                for source in range(gz):
                    def await_edge(dy=dy, dx=dx, source=source):
                        pltpu.make_async_remote_copy(
                            src_ref=payload(dy),
                            dst_ref=slot(True, dy, source),
                            send_sem=x1_send.at[1 + dy, 0],
                            recv_sem=x1_recv.at[1 + dy, source],
                            device_id=device(source, dy, dx),
                            device_id_type=MESH,
                        ).wait_recv()
                    pl.when(ok)(await_edge)

    for ok, make in sends:
        when(ok, lambda make=make: make().wait_send())


def layers_kernel(
    sizes, shape, where_ref, m1, x1, my, xy, narrow_ref, wide_ref, first_ref, second_ref, head_ref, packed, taps, taps_high, taps_low, product, fix
):
    gz, gy, gx = sizes
    bz, by, bx = shape
    depth = gz * bz
    slab = bx // gz
    out_lanes = by * slab
    tiles = taps.shape[0]
    me, at_y, at_x = where_ref[0], where_ref[1], where_ref[2]
    low_slab = me == 0
    high_slab = me == gz - 1
    taps[...] = jnp.zeros(taps.shape, F32)
    for plane in (0, depth + 1):
        product[plane] = jnp.zeros(product.shape[1:], F32)
    fix[...] = jnp.zeros(fix.shape, F32)
    first_left = left_rows(narrow_ref[0:96, :])
    second_left = left_rows(
        jnp.concatenate([wide_ref[48 * a : 48 * a + 32, :] for a in range(3)], axis=0)
    )
    first_bias = jnp.concatenate([column(first_ref)] * 3, axis=0)
    second_bias = column(second_ref)
    head = column(head_ref)
    shape = (48, tiles * LANES)
    lane, row = lane_of(shape), row_of(shape)
    place_y = at_y * by + lane // slab - 1
    place_x = at_x * bx + me * slab + lane % slab + row // 16 - 1
    inside = (place_y >= 0) & (place_y < gy * by) & (place_x >= 0) & (place_x < gx * bx)
    mask = jnp.where(inside, 1.0, 0.0).astype(F32)

    lane = lane_of((depth, LANES))
    take_edge = (low_slab & (lane >= bx - 2)) | (high_slab & (lane < 2))
    windows = []
    turn = lax.rem(2 - me * slab + bx, bx)
    for line in range(by + 4):
        rows = []
        for source, beside in ((m1, my), (x1, xy)):
            if 2 <= line < by + 2:
                rows.append(source[pl.ds(line - 2, depth, stride=by), :])
            else:
                side, place = (0, line) if line < 2 else (1, line - by - 2)
                rows.append(beside[side, pl.ds(place, depth, stride=2), :])
        windows.append(pltpu.roll(jnp.where(take_edge, rows[1], rows[0]), turn, 1))
    wide_tiles = -(-(by + 4) * slab // LANES)
    for s in range(5):
        strips = []
        for tile in range(wide_tiles):
            strip = jnp.zeros((depth, LANES), F32)
            for line in range(by + 4):
                if line * slab // LANES == tile:
                    begin = line * slab % LANES
                    piece = pltpu.roll(windows[line], (begin - s) % LANES, 1)
                    strip = jnp.where((lane >= begin) & (lane < begin + slab), piece, strip)
            strips.append(strip)
        strips.append(jnp.zeros((depth, LANES), F32))
        for b in range(3):
            for tile in range(tiles):
                jump, off = divmod(b * slab, LANES)
                value = strips[min(tile + jump, wide_tiles)]
                if off:
                    after = strips[min(tile + jump + 1, wide_tiles)]
                    value = jnp.where(
                        lane < LANES - off,
                        pltpu.roll(value, LANES - off, 1),
                        pltpu.roll(after, LANES - off, 1),
                    )
                taps[tile, pl.ds(16 + b * 5 + s, depth, stride=16), :] = value
    high, low = split(taps[...])
    taps_high[...] = high
    taps_low[...] = low

    def forward(z, hidden):
        rows = pl.ds(aligned(z * 16, 16), 48)
        high = jnp.concatenate([taps_high[t, rows, :] for t in range(tiles)], axis=1)
        low = jnp.concatenate([taps_low[t, rows, :] for t in range(tiles)], axis=1)
        pre = mxu(first_left, right_rows(high, low))
        cand = jnp.tanh(pre[0:48])
        change = jax.nn.sigmoid(pre[48:96] + first_bias)
        hidden = hidden + change * (mask * cand - hidden)
        field = jnp.concatenate(
            [hidden[:, b * slab : b * slab + out_lanes] for b in range(3)], axis=0
        )
        high, low = split(field)
        product[z + 1] = mxu(second_left, right_rows(high, low))
        return hidden

    times(depth, forward, jnp.zeros((48, tiles * LANES), F32))

    def back(z, hidden):
        pre = product[z, 0:32] + product[z + 1, 32:64] + product[z + 2, 64:96]
        cand = jnp.tanh(pre[0:16])
        change = jax.nn.sigmoid(pre[16:32] + second_bias)
        hidden = hidden + change * (cand - hidden)
        fix[pl.ds(z + 2, 1), 0:out_lanes] = jnp.sum(head * hidden, axis=0, keepdims=True)
        return hidden

    times(depth, back, jnp.zeros((16, out_lanes), F32), True)
    for tile in range(-(-out_lanes // LANES)):
        lanes = slice(tile * LANES, (tile + 1) * LANES)
        centre = taps[tile, pl.ds(16 + 12, depth, stride=16), :]
        fix[2 : 2 + depth, lanes] = fix[2 : 2 + depth, lanes] + centre
    for target in range(gz):
        packed[target] = fix[bz * target : bz * target + bz + 4, :]


def scatter_kernel(sizes, by, slab, packed, m3, x3, m3_send, m3_recv, x3_send, x3_recv):
    gz, gy, gx = sizes
    me = lax.axis_index("gz")
    at_y = lax.axis_index("gy")
    at_x = lax.axis_index("gx")
    low_slab = me == 0
    high_slab = me == gz - 1

    def exists(dy, dx):
        ok = None
        for where, step, count in ((at_y, dy, gy), (at_x, dx, gx)):
            if step == 0:
                continue
            here = where > 0 if step < 0 else where < count - 1
            ok = here if ok is None else ok & here
        return ok

    def when(ok, action):
        if ok is None:
            action()
        else:
            pl.when(ok)(action)

    def device(z, dy, dx):
        return {
            "win": lax.axis_index("win"),
            "gz": z,
            "gy": lax.rem(at_y + dy + gy, gy),
            "gx": lax.rem(at_x + dx + gx, gx),
        }

    def peer(k):
        return lax.rem(me + k, gz)

    steps_y = (0,) + ((-1, 1) if gy > 1 else ())
    steps_x = (0,) + ((-1, 1) if gx > 1 else ())

    barrier = pltpu.get_barrier_semaphore()
    for dy in steps_y:
        for dx in steps_x:
            for k in range(gz):
                if (dy, dx, k) != (0, 0, 0):
                    def greet(dy=dy, dx=dx, k=k):
                        pl.semaphore_signal(
                            barrier, inc=1, device_id=device(peer(k), dy, dx), device_id_type=MESH
                        )
                    when(exists(dy, dx), greet)
    span_y = 1 + (at_y > 0).astype(jnp.int32) + (at_y < gy - 1).astype(jnp.int32)
    span_x = 1 + (at_x > 0).astype(jnp.int32) + (at_x < gx - 1).astype(jnp.int32)
    pl.semaphore_wait(barrier, gz * span_y * span_x - 1)

    lanes = packed.shape[2]
    last = (by - 2) * slab // LANES * LANES

    def part(dy):
        return {0: slice(0, lanes), 1: slice(last, last + LANES), -1: slice(0, LANES)}[dy]

    def clean_middle(dy, k):
        target = peer(k)
        return pltpu.make_async_remote_copy(
            src_ref=packed.at[target, :, part(dy)],
            dst_ref=m3.at[1 - dy, me, :, part(dy)],
            send_sem=m3_send.at[dy + 1, k],
            recv_sem=m3_recv.at[1 - dy, me],
            device_id=device(target, dy, 0),
            device_id_type=MESH,
        )

    def clean_edge(dy, dx, k):
        target = peer(k)
        side = (dx + 1) // 2
        return pltpu.make_async_remote_copy(
            src_ref=packed.at[target, :, part(dy)],
            dst_ref=x3.at[1 - dy, 1 - side, :, part(dy)],
            send_sem=x3_send.at[dy + 1, side, k],
            recv_sem=x3_recv.at[1 - dy, 1 - side],
            device_id=device(target, dy, dx),
            device_id_type=MESH,
        )

    late = []
    for dy in steps_y:
        for k in range(gz - 1, -1, -1):
            if (dy, k) != (0, 0):
                late.append((exists(dy, 0), functools.partial(clean_middle, dy, k)))
    for dy in steps_y:
        for dx in steps_x:
            if dx != 0:
                ok = exists(dy, dx) & (high_slab if dx > 0 else low_slab)
                for k in range(gz):
                    late.append((ok, functools.partial(clean_edge, dy, dx, k)))
    for ok, make in late:
        when(ok, lambda make=make: make().start())
    m3[1, me] = packed[me]
    for index, ok in ((0, at_y == 0), (2, at_y == gy - 1)):
        def no_row_again(index=index):
            m3[index] = jnp.zeros(m3.shape[1:], F32)
            x3[index] = jnp.zeros(x3.shape[1:], F32)
        pl.when(ok)(no_row_again)
    for side, ok in ((0, at_x == 0), (1, at_x == gx - 1)):
        def no_side(side=side):
            for index in range(3):
                x3[index, side] = jnp.zeros(x3.shape[2:], F32)
        pl.when(ok)(no_side)
    for dy in steps_y:
        for k in range(gz):
            if (dy, k) != (0, 0):
                source = peer(k)
                def await_clean(dy=dy, source=source):
                    pltpu.make_async_remote_copy(
                        src_ref=packed.at[0, :, part(-dy)],
                        dst_ref=m3.at[1 + dy, source, :, part(-dy)],
                        send_sem=m3_send.at[1 + dy, 0],
                        recv_sem=m3_recv.at[1 + dy, source],
                        device_id=device(source, dy, 0),
                        device_id_type=MESH,
                    ).wait_recv()
                when(exists(dy, 0), await_clean)
    for dy in steps_y:
        for dx in steps_x:
            if dx != 0:
                side = (dx + 1) // 2
                source = gz - 1 if dx < 0 else 0
                def await_side(dy=dy, dx=dx, side=side, source=source):
                    pltpu.make_async_remote_copy(
                        src_ref=packed.at[0, :, part(-dy)],
                        dst_ref=x3.at[1 + dy, side, :, part(-dy)],
                        send_sem=x3_send.at[1 + dy, side, 0],
                        recv_sem=x3_recv.at[1 + dy, side],
                        device_id=device(source, dy, dx),
                        device_id_type=MESH,
                    ).wait_recv()
                when(exists(dy, dx), await_side)

    for ok, make in late:
        when(ok, lambda make=make: make().wait_send())


def segment_kernel(
    sizes,
    where_ref,
    m3,
    x3,
    narrow_ref,
    wide_ref,
    in_ref,
    last_ref,
    clean_ref,
    out_ref,
    middle_ref,
    edge_ref,
    taps,
    result,
):
    gz, gy, gx = sizes
    lines, planes, bx = middle_ref.shape
    by, bz = lines - 4, planes - 4
    me, at_y, at_x = where_ref[0], where_ref[1], where_ref[2]
    slab = bx // gz
    lane = lane_of((bz + 4, LANES))
    for line in range(by + 4):
        index, y = (0, by - 2 + line) if line < 2 else (1, line - 2) if line < by + 2 else (2, line - by - 2)
        tile, off = divmod(y * slab, LANES)
        lanes = slice(tile * LANES, (tile + 1) * LANES)
        whole = jnp.zeros((bz + 4, LANES), F32)
        for source in range(gz):
            begin = source * slab
            piece = pltpu.roll(m3[index, source, :, lanes], (begin - off) % LANES, 1)
            whole = jnp.where((lane >= begin) & (lane < begin + slab), piece, whole)
        middle_ref[line] = whole
        before = pltpu.roll(x3[index, 0, :, lanes], (bx - off - slab) % LANES, 1)
        after = pltpu.roll(x3[index, 1, :, lanes], (-off) % LANES, 1)
        edge_ref[line] = jnp.where(lane < LANES // 2, after, before)

    in_left = left_rows(narrow_ref[96:144, :])
    out_left = left_rows(
        jnp.concatenate([wide_ref[48 * a + 32 : 48 * a + 48, :] for a in range(3)], axis=0)
    )
    in_bias = jnp.concatenate([column(in_ref)] * 3, axis=0)
    out_bias = column(last_ref)
    for y in range(by + 2):
        taps[y, pl.ds(15, planes, stride=16), :] = jnp.zeros((planes, bx), F32)
    lane = lane_of((planes, bx))
    for line in range(lines):
        middle, edge = middle_ref[line], edge_ref[line]
        for s in range(5):
            value = middle
            if s < 2:
                value = pltpu.roll(jnp.where(lane >= bx - (2 - s), edge, middle), 2 - s, 1)
            if s > 2:
                value = pltpu.roll(jnp.where(lane < s - 2, edge, middle), bx - (s - 2), 1)
            for b in range(3):
                if 0 <= line - b < by + 2:
                    taps[line - b, pl.ds(b * 5 + s, planes, stride=16), :] = value

    for z in range(bz):
        clean_ref[z] = middle_ref[2 : 2 + by, 2 + z, :]
    shape = (48, (by + 2) * bx)
    lane, row = lane_of(shape), row_of(shape)
    place_y = at_y * by + lane // bx - 1
    place_x = at_x * bx + lane % bx + row // 16 - 1
    inside = (place_y >= 0) & (place_y < gy * by) & (place_x >= 0) & (place_x < gx * bx)
    mask = jnp.where(inside, 1.0, 0.0).astype(F32)
    partial = []
    for z in range(bz + 2):
        rows = jnp.concatenate([taps[y, z * 16 : z * 16 + 48, :] for y in range(by + 2)], axis=1)
        high, low = split(rows)
        grown = jnp.maximum(mxu(in_left, right_rows(high, low)) + in_bias, 0.0) * mask
        if z == 0:
            grown = grown * jnp.where(me > 0, 1.0, 0.0).astype(F32)
        if z == bz + 1:
            grown = grown * jnp.where(me < gz - 1, 1.0, 0.0).astype(F32)
        high, low = split(grown)
        field_high = jnp.concatenate([high[:, b * bx : (b + by) * bx] for b in range(3)], axis=0)
        field_low = jnp.concatenate([low[:, b * bx : (b + by) * bx] for b in range(3)], axis=0)
        partial.append(mxu(out_left, right_rows(field_high, field_low)))
        if z >= 2:
            total = partial[z - 2][0:16] + partial[z - 1][16:32] + partial[z][32:48] + out_bias
            for y in range(by):
                result[pl.ds((z - 2) * by + y, 16, stride=bz * by), :] = total[:, y * bx : (y + 1) * bx]
    out_ref[...] = result[0 : 16 * bz * by, :]


def narrow_rows(weight):
    parts = weight.shape[0] // 16
    kernel = weight.reshape(parts, 16, 3, 3, 3)
    moved = jnp.stack(
        [jnp.pad(kernel, ((0, 0),) * 4 + ((c, 2 - c),)) for c in range(3)], axis=1
    ).reshape(parts * 48, 3, 15)
    return jnp.pad(moved, ((0, 0), (0, 0), (0, 1))).reshape(parts * 48, 48)


def wide_rows(weight):
    outs, ins = weight.shape[0], weight.shape[1]
    return weight.reshape(outs, ins, 3, 9).transpose(2, 0, 3, 1).reshape(3 * outs, 9 * ins)


def body(sizes, noisy, first_weight, first_bias, second_weight, second_bias, head_weight,
         seg_weight_in, seg_bias_in, seg_weight_out, seg_bias_out):
    gz, gy, gx = sizes
    bz, by, bx = noisy.shape
    depth = gz * bz
    slab = bx // gz
    tiles = -(-(by + 2) * slab // LANES)
    out_lanes = by * slab
    out_tiles = -(-out_lanes // LANES)
    narrow = narrow_rows(jnp.concatenate([first_weight, seg_weight_in], axis=0))
    wide = wide_rows(jnp.concatenate([second_weight, seg_weight_out], axis=0))
    rows = [v.reshape(1, -1) for v in (first_bias, second_bias, head_weight, seg_bias_in, seg_bias_out)]
    vmem = pl.BlockSpec(memory_space=pltpu.VMEM)
    dma = pltpu.SemaphoreType.DMA
    smem = pl.BlockSpec(memory_space=pltpu.SMEM)
    blocks = jax.ShapeDtypeStruct((gz, bz * by, bx), F32)
    halos = jax.ShapeDtypeStruct((2, gz, bz * 2, bx), F32)
    m1, x1, my, xy, where = pl.pallas_call(
        functools.partial(gather_kernel, sizes, by),
        out_shape=[blocks, blocks, halos, halos, jax.ShapeDtypeStruct((3,), jnp.int32)],
        in_specs=[vmem],
        out_specs=[vmem] * 4 + [smem],
        scratch_shapes=[
            pltpu.VMEM((2, bz * 2, bx), F32), dma((3, gz)), dma((3, gz)), dma((3, 2)), dma((3, gz))
        ],
        compiler_params=pltpu.CompilerParams(collective_id=0, has_side_effects=True),
        name="gather",
    )(noisy.reshape(bz * by, bx))
    packed = pl.pallas_call(
        functools.partial(layers_kernel, sizes, (bz, by, bx)),
        out_shape=jax.ShapeDtypeStruct((gz, bz + 4, out_tiles * LANES), F32),
        in_specs=[smem] + [vmem] * 9,
        out_specs=vmem,
        scratch_shapes=[
            pltpu.VMEM((tiles, (depth + 2) * 16, LANES), F32),
            pltpu.VMEM((tiles, (depth + 2) * 16, LANES), BF16),
            pltpu.VMEM((tiles, (depth + 2) * 16, LANES), BF16),
            pltpu.VMEM((depth + 2, 96, out_lanes), F32),
            pltpu.VMEM((depth + 16, out_tiles * LANES), F32),
        ],
        name="layers",
    )(
        where,
        m1.reshape(depth * by, bx),
        x1.reshape(depth * by, bx),
        my.reshape(2, depth * 2, bx),
        xy.reshape(2, depth * 2, bx),
        narrow,
        wide,
        *rows[:3],
    )
    m3, x3 = pl.pallas_call(
        functools.partial(scatter_kernel, sizes, by, slab),
        out_shape=[
            jax.ShapeDtypeStruct((3, gz, bz + 4, out_tiles * LANES), F32),
            jax.ShapeDtypeStruct((3, 2, bz + 4, out_tiles * LANES), F32),
        ],
        in_specs=[vmem],
        out_specs=[vmem] * 2,
        scratch_shapes=[dma((3, gz)), dma((3, gz)), dma((3, 2, gz)), dma((3, 2))],
        compiler_params=pltpu.CompilerParams(collective_id=1, has_side_effects=True),
        name="scatter",
    )(packed)
    clean, features = pl.pallas_call(
        functools.partial(segment_kernel, sizes),
        out_shape=[
            jax.ShapeDtypeStruct((bz, by, bx), F32),
            jax.ShapeDtypeStruct((16 * bz * by, bx), F32),
        ],
        in_specs=[smem] + [vmem] * 6,
        out_specs=[vmem] * 2,
        scratch_shapes=[
            pltpu.VMEM((by + 4, bz + 4, bx), F32),
            pltpu.VMEM((by + 4, bz + 4, bx), F32),
            pltpu.VMEM((by + 2, (bz + 5) * 16, bx), F32),
            pltpu.VMEM((17 * bz * by, bx), F32),
        ],
        name="segment",
    )(where, m3, x3, narrow, wide, *rows[3:])
    return clean, features.reshape(16, bz, by, bx)


def solution(mesh):
    sizes = (mesh.shape["gz"], mesh.shape["gy"], mesh.shape["gx"])
    in_specs = (P(("win", "gz"), "gy", "gx"), P(), P(), P(), P(), P(), P(), P(), P(), P())
    out_specs = (P(("win", "gz"), "gy", "gx"), P(None, ("win", "gz"), "gy", "gx"))
    return jax.shard_map(
        functools.partial(body, sizes), mesh=mesh, in_specs=in_specs, out_specs=out_specs, check_vma=False
    )
```

profile of v0, /device:TPU:0, one launch (start us, length us, event | category | flops | bytes accessed | tf_op | source)
XLA Modules:
  0.0 32.6 jit_solution(4151272656552947549)
XLA Ops:
  0.6 0.0 copy-start.2
  0.6 0.8 %copy.16 = f32[16,1,27]{0,1,2:T(1,128)S(1)} copy(f32[16,1,27]{2,1,0:T(1,128)} %param.16) | data formatting | bytes 3456 | tf_op args[6]
  1.4 0.0 copy-done.2
  1.4 0.1 maximum_reduce_fusion
  1.6 0.1 reshape.57
  1.7 0.1 copy.17
  1.8 0.1 copy.18
  1.9 0.2 pad_maximum_fusion
  2.2 0.2 reshape.58
  2.3 0.0 copy-start.1
  2.3 0.7 %copy.21.narrow_ref = f32[144,48]{1,0:T(8,128)} copy(f32[144,48]{0,1:T(8,128)S(1)} %bitcast.30) | data formatting | bytes 55296 | tf_op jit(solution)/shard_map/reshape | solution.py:543
  3.1 0.0 copy-start
  3.1 11.3 %gather.1 = (f32[4,32,128]{2,1,0:T(8,128)}, f32[4,32,128]{2,1,0:T(8,128)}, f32[2,4,8,128]{3,2,1,0:T(8,128)}, f32[2,4,8,128]{3,2,1,0:T(8,128)}, s32[3]{0:T(128)}) custom-call(f32[32,128]{1,0:T(8,128)} %bitcast.35), custom_call_target="tpu_custom_call" | custom-call | tf_op jit(solution)/shard_map/gather/pallas_call | solution.py:568
  14.4 0.0 copy-done.1
  14.4 0.2 copy.19
  14.6 0.0 copy-done
  14.6 0.1 pad_maximum_fusion.1
  14.8 0.1 copy.26
  14.9 0.2 reshape.61
  15.1 0.8 %copy.22.wide_ref = f32[144,144]{1,0:T(8,128)} copy(f32[144,144]{0,1:T(8,128)S(1)} %reshape.61) | data formatting | bytes 165888 | tf_op jit(solution)/shard_map/reshape | solution.py:548
  15.8 4.1 %layers.1.packed = f32[4,8,256]{2,1,0:T(8,128)} custom-call(s32[3]{0:T(128)} %get-tuple-element.11.where_ref, f32[128,128]{1,0:T(8,128)} %bitcast.31, f32[128,128]{1,0:T(8,128)} %bitcast.32, f32[2,32,128]{2,1,0:T(8,128)} %bitcast.33, f32[2,32,128]{2,1,0:T(8,128)} %bitcast.34, f32[144,48]{1,0:T(8,128)} %copy.21.narrow_ref, f32[144,144]{1,0:T(8,128)} %copy.22.wide_ref, ...), custom_call_target="tpu_custom_call" | custom-call | tf_op jit(solution)/shard_map/layers/pallas_call | solution.py:579
  19.9 8.6 %scatter.1 = (f32[3,4,8,256]{3,2,1,0:T(8,128)}, f32[3,2,8,256]{3,2,1,0:T(8,128)}) custom-call(f32[4,8,256]{2,1,0:T(8,128)} %layers.1.packed), custom_call_target="tpu_custom_call" | custom-call | tf_op jit(solution)/shard_map/scatter/pallas_call | solution.py:602
  28.6 4.0 %segment.1 = (f32[4,8,128]{2,1,0:T(8,128)}, f32[512,128]{1,0:T(8,128)}) custom-call(s32[3]{0:T(128)} %get-tuple-element.11.where_ref, f32[3,4,8,256]{3,2,1,0:T(8,128)} %get-tuple-element.16.m3, f32[3,2,8,256]{3,2,1,0:T(8,128)} %get-tuple-element.17.x3, f32[144,48]{1,0:T(8,128)} %copy.21.narrow_ref, f32[144,144]{1,0:T(8,128)} %copy.22.wide_ref, ...), custom_call_target="tpu_custom_call" | custom-call | tf_op jit(solution)/shard_map/segment/pallas_call | solution.py:614
  (3 shorter events, 0.1 us)
Async XLA Ops:
  0.6 0.8 %copy-start.2 = (f32[32,1,27]{0,1,2:T(1,128)S(1)}, f32[32,1,27]{0,1,2:T(1,128)}, u32[]{:S(2)}) copy-start(f32[32,1,27]{0,1,2:T(1,128)} %param.11) | copy-start | bytes 10372
  2.3 12.1 %copy-start.1 = (f32[16,16,27]{2,1,0:T(8,128)S(1)}, f32[16,16,27]{2,1,0:T(8,128)}, u32[]{:S(2)}) copy-start(f32[16,16,27]{2,1,0:T(8,128)} %param.18) | copy-start | bytes 82948
  3.1 11.6 %copy-start = (f32[32,16,27]{0,1,2:T(8,128)S(1)}, f32[32,16,27]{0,1,2:T(8,128)}, u32[]{:S(2)}) copy-start(f32[32,16,27]{0,1,2:T(8,128)} %param.13) | copy-start | bytes 165892
where the time goes:
time: 32.9 us; the launch traced here: 32.6 us
  Pallas kernels  28.1 us (85%)
  local copies, waits for them, and re-layouts  3.24 us (10%)
  between operations  0.75 us (2%)
  other arithmetic  0.49 us (1%)
    pallas_call x1, Pallas kernels, body(): pl.pallas_call(functools.partial(gather_kernel, sizes, by), out_shape=[bl...  11.3 us
    pallas_call x1, Pallas kernels, body(): pl.pallas_call(functools.partial(scatter_kernel, sizes, by, slab), out_sh...  8.62 us
    pallas_call x1, Pallas kernels, body(): pl.pallas_call(functools.partial(layers_kernel, sizes, (bz, by, bx)), out...  4.12 us
    pallas_call x1, Pallas kernels, body(): pl.pallas_call(functools.partial(segment_kernel, sizes), out_shape=[jax.S...  4.03 us
    reshape x3, local copies, waits for them, and re-layouts, wide_rows(): weight.reshape(outs, ins, 3, 9).transpose(2, 0, 3, 1)  1.03 us
    unnamed x8, local copies, waits for them, and re-layouts  0.99 us
    reshape x1, local copies, waits for them, and re-layouts, narrow_rows(): return jnp.pad(moved, ((0, 0), (0, 0), (0, 1))).reshape(parts * 48, 48)  0.73 us

commit v1 on v0

--- a/solution.py
+++ b/solution.py
@@ -58,14 +58,80 @@
     return start if isinstance(start, int) else pl.multiple_of(start, unit)
 
 
-def gather_kernel(sizes, by, noisy_ref, m1, x1, my, xy, where_ref, halo, m1_send, m1_recv, x1_send, x1_recv):
+def matches(left, right):
+    return jnp.where(left == right, 1.0, 0.0).astype(BF16)
+
+
+def spread_narrow(weight, shift):
+    taps = weight.shape[1]
+    shape = (taps, 48)
+    tap, col = row_of(shape), lane_of(shape)
+    plane = (tap >= 9).astype(jnp.int32) + (tap >= 18).astype(jnp.int32)
+    rest = tap - 9 * plane
+    line = (rest >= 3).astype(jnp.int32) + (rest >= 6).astype(jnp.int32)
+    place = matches(col, tap + 7 * plane + 2 * line + shift)
+    return tuple(mxu(part, place).astype(BF16) for part in split(weight))
+
+
+def narrow_left(weight):
+    parts = weight.shape[0] // 16
+    highs, lows = [], []
+    for part in range(parts):
+        for shift in range(3):
+            high, low = spread_narrow(weight[16 * part : 16 * part + 16], shift)
+            highs.append(high)
+            lows.append(low)
+    high, low = jnp.concatenate(highs, axis=0), jnp.concatenate(lows, axis=0)
+    return jnp.concatenate([high, high, low], axis=1)
+
+
+def wide_left(turned):
+    flat = turned.T
+    taps = flat.shape[1] // 3
+    return left_rows(
+        jnp.concatenate([flat[:, taps * a : taps * (a + 1)] for a in range(3)], axis=0)
+    )
+
+
+def last_left(weight):
+    outs, ins, taps = weight.shape
+    shape = (taps, taps * ins)
+    place = matches(row_of(shape), lane_of(shape) // ins)
+    shape = (outs * ins, taps * ins)
+    keep = (row_of(shape) % ins) == (lane_of(shape) % ins)
+    shape = (outs, outs * ins)
+    gather = matches(row_of(shape), lane_of(shape) // ins)
+    parts = []
+    for part in split(weight.reshape(outs * ins, taps)):
+        grown = jnp.where(keep, mxu(part, place), 0.0).astype(BF16)
+        parts.append(mxu(gather, grown).astype(BF16))
+    third = taps * ins // 3
+    high, low = (
+        jnp.concatenate([p[:, third * a : third * (a + 1)] for a in range(3)], axis=0) for p in parts
+    )
+    return jnp.concatenate([high, high, low], axis=1)
+
+
+def whole_kernel(
+    sizes, bz, by, bx,
+    noisy_any, w1_any, b1_any, w2_any, b2_any, head_any, w3_any, b3_any, w4_any, b4_any,
+    clean_ref, out_ref,
+    noisy_ref, w1_ref, b1_ref, w2_ref, b2_ref, head_ref, w3_ref, b3_ref, w4_ref, b4_ref, load_sem,
+    m1, x1, my, xy, halo, m1_send, m1_recv, x1_send, x1_recv,
+    wide_taps, taps_high, taps_low, product, fix, packed,
+    m3, x3, m3_send, m3_recv, x3_send, x3_recv,
+    middle_ref, edge_ref, seg_taps, result,
+):
     gz, gy, gx = sizes
+    depth = gz * bz
+    slab = bx // gz
+    out_lanes = by * slab
+    tiles = wide_taps.shape[0]
     me = lax.axis_index("gz")
     at_y = lax.axis_index("gy")
     at_x = lax.axis_index("gx")
     low_slab = me == 0
     high_slab = me == gz - 1
-
     def exists(dy, dx):
         ok = None
         for where, step, count in ((at_y, dy, gy), (at_x, dx, gx)):
@@ -95,18 +161,32 @@
     steps_y = (0,) + ((-1, 1) if gy > 1 else ())
     steps_x = (0,) + ((-1, 1) if gx > 1 else ())
 
-    for side, first in ((0, 0), (1, by - 2)):
-        for z in range(noisy_ref.shape[0] // by):
-            halo[side, 2 * z : 2 * z + 2, :] = noisy_ref[z * by + first : z * by + first + 2, :]
-
     def payload(dy):
         return noisy_ref if dy == 0 else halo.at[(dy + 1) // 2]
 
     def slot(edge, dy, z):
         if dy == 0:
-            return (x1 if edge else m1).at[z]
-        return (xy if edge else my).at[(dy + 1) // 2, z]
-
+            return (x1 if edge else m1).at[pl.ds(aligned(z * bz * by, bz * by), bz * by), :]
+        return (xy if edge else my).at[(dy + 1) // 2, pl.ds(aligned(z * bz * 2, bz * 2), bz * 2), :]
+
+    loads = [
+        pltpu.make_async_copy(source, target, load_sem.at[i])
+        for i, (source, target) in enumerate(
+            (
+                (noisy_any, noisy_ref),
+                (w1_any.at[:, 0, :], w1_ref),
+                (w2_any, w2_ref),
+                (w3_any.at[:, 0, :], w3_ref),
+                (w4_any, w4_ref),
+                (b1_any, b1_ref),
+                (b2_any, b2_ref),
+                (head_any, head_ref),
+                (b3_any, b3_ref),
+                (b4_any, b4_ref),
+            )
+        )
+    ]
+    loads[0].start()
     barrier = pltpu.get_barrier_semaphore()
     for dy in steps_y:
         for dx in steps_x:
@@ -117,6 +197,13 @@
                             barrier, inc=1, device_id=device(peer(k), dy, dx), device_id_type=MESH
                         )
                     when(exists(dy, dx), greet)
+    for load in loads[1:]:
+        load.start()
+    loads[0].wait()
+    for side, first in ((0, 0), (1, by - 2)):
+        for z in range(noisy_ref.shape[0] // by):
+            halo[side, 2 * z : 2 * z + 2, :] = noisy_ref[z * by + first : z * by + first + 2, :]
+
     span_y = 1 + (at_y > 0).astype(jnp.int32) + (at_y < gy - 1).astype(jnp.int32)
     span_x = 1 + (at_x > 0).astype(jnp.int32) + (at_x < gx - 1).astype(jnp.int32)
     pl.semaphore_wait(barrier, gz * span_y * span_x - 1)
@@ -156,14 +243,11 @@
     for ok, make in sends:
         when(ok, lambda make=make: make().start())
 
-    for i, value in enumerate((me, at_y, at_x)):
-        where_ref[i] = value
-    m1[me] = noisy_ref[...]
+    m1[pl.ds(aligned(me * bz * by, bz * by), bz * by), :] = noisy_ref[...]
     for index, ok in ((0, at_y == 0), (1, at_y == gy - 1)):
         def no_row(index=index):
-            for z in range(gz):
-                my[index, z] = jnp.zeros(my.shape[2:], F32)
-                xy[index, z] = jnp.zeros(xy.shape[2:], F32)
+            my[index] = jnp.zeros(my.shape[1:], F32)
+            xy[index] = jnp.zeros(xy.shape[1:], F32)
         pl.when(ok)(no_row)
     no_edge = jnp.logical_not((low_slab & (at_x > 0)) | (high_slab & (at_x < gx - 1)))
 
@@ -172,6 +256,29 @@
         xy[...] = jnp.zeros(xy.shape, F32)
 
     pl.when(no_edge)(no_neighbour)
+    for load in loads[1:]:
+        load.wait()
+    wide_taps[...] = jnp.zeros(wide_taps.shape, F32)
+    for plane in (0, depth + 1):
+        product[plane] = jnp.zeros(product.shape[1:], F32)
+    fix[...] = jnp.zeros(fix.shape, F32)
+    turned = w1_ref[...].T
+    first_left = narrow_left(turned)
+    second_left = wide_left(w2_ref[...].reshape(-1, w2_ref.shape[2]))
+    in_left = narrow_left(w3_ref[...])
+    out_left = last_left(w4_ref[...])
+    in_bias = jnp.concatenate([column(b3_ref)] * 3, axis=0)
+    out_bias = column(b4_ref)
+    first_bias = jnp.concatenate([column(b1_ref)] * 3, axis=0)
+    second_bias = column(b2_ref)
+    head = column(head_ref)
+    shape = (48, tiles * LANES)
+    lane, row = lane_of(shape), row_of(shape)
+    place_y = at_y * by + lane // slab - 1
+    place_x = at_x * bx + me * slab + lane % slab + row // 16 - 1
+    inside = (place_y >= 0) & (place_y < gy * by) & (place_x >= 0) & (place_x < gx * bx)
+    mask = jnp.where(inside, 1.0, 0.0).astype(F32)
+
     for dy in steps_y:
         for k in range(gz):
             if (dy, k) != (0, 0):
@@ -201,40 +308,6 @@
                             device_id_type=MESH,
                         ).wait_recv()
                     pl.when(ok)(await_edge)
-
-    for ok, make in sends:
-        when(ok, lambda make=make: make().wait_send())
-
-
-def layers_kernel(
-    sizes, shape, where_ref, m1, x1, my, xy, narrow_ref, wide_ref, first_ref, second_ref, head_ref, packed, taps, taps_high, taps_low, product, fix
-):
-    gz, gy, gx = sizes
-    bz, by, bx = shape
-    depth = gz * bz
-    slab = bx // gz
-    out_lanes = by * slab
-    tiles = taps.shape[0]
-    me, at_y, at_x = where_ref[0], where_ref[1], where_ref[2]
-    low_slab = me == 0
-    high_slab = me == gz - 1
-    taps[...] = jnp.zeros(taps.shape, F32)
-    for plane in (0, depth + 1):
-        product[plane] = jnp.zeros(product.shape[1:], F32)
-    fix[...] = jnp.zeros(fix.shape, F32)
-    first_left = left_rows(narrow_ref[0:96, :])
-    second_left = left_rows(
-        jnp.concatenate([wide_ref[48 * a : 48 * a + 32, :] for a in range(3)], axis=0)
-    )
-    first_bias = jnp.concatenate([column(first_ref)] * 3, axis=0)
-    second_bias = column(second_ref)
-    head = column(head_ref)
-    shape = (48, tiles * LANES)
-    lane, row = lane_of(shape), row_of(shape)
-    place_y = at_y * by + lane // slab - 1
-    place_x = at_x * bx + me * slab + lane % slab + row // 16 - 1
-    inside = (place_y >= 0) & (place_y < gy * by) & (place_x >= 0) & (place_x < gx * bx)
-    mask = jnp.where(inside, 1.0, 0.0).astype(F32)
 
     lane = lane_of((depth, LANES))
     take_edge = (low_slab & (lane >= bx - 2)) | (high_slab & (lane < 2))
@@ -272,8 +345,8 @@
                         pltpu.roll(value, LANES - off, 1),
                         pltpu.roll(after, LANES - off, 1),
                     )
-                taps[tile, pl.ds(16 + b * 5 + s, depth, stride=16), :] = value
-    high, low = split(taps[...])
+                wide_taps[tile, pl.ds(16 + b * 5 + s, depth, stride=16), :] = value
+    high, low = split(wide_taps[...])
     taps_high[...] = high
     taps_low[...] = low
 
@@ -305,68 +378,17 @@
     times(depth, back, jnp.zeros((16, out_lanes), F32), True)
     for tile in range(-(-out_lanes // LANES)):
         lanes = slice(tile * LANES, (tile + 1) * LANES)
-        centre = taps[tile, pl.ds(16 + 12, depth, stride=16), :]
+        centre = wide_taps[tile, pl.ds(16 + 12, depth, stride=16), :]
         fix[2 : 2 + depth, lanes] = fix[2 : 2 + depth, lanes] + centre
     for target in range(gz):
         packed[target] = fix[bz * target : bz * target + bz + 4, :]
 
 
-def scatter_kernel(sizes, by, slab, packed, m3, x3, m3_send, m3_recv, x3_send, x3_recv):
-    gz, gy, gx = sizes
-    me = lax.axis_index("gz")
-    at_y = lax.axis_index("gy")
-    at_x = lax.axis_index("gx")
-    low_slab = me == 0
-    high_slab = me == gz - 1
-
-    def exists(dy, dx):
-        ok = None
-        for where, step, count in ((at_y, dy, gy), (at_x, dx, gx)):
-            if step == 0:
-                continue
-            here = where > 0 if step < 0 else where < count - 1
-            ok = here if ok is None else ok & here
-        return ok
-
-    def when(ok, action):
-        if ok is None:
-            action()
-        else:
-            pl.when(ok)(action)
-
-    def device(z, dy, dx):
-        return {
-            "win": lax.axis_index("win"),
-            "gz": z,
-            "gy": lax.rem(at_y + dy + gy, gy),
-            "gx": lax.rem(at_x + dx + gx, gx),
-        }
-
-    def peer(k):
-        return lax.rem(me + k, gz)
-
-    steps_y = (0,) + ((-1, 1) if gy > 1 else ())
-    steps_x = (0,) + ((-1, 1) if gx > 1 else ())
-
-    barrier = pltpu.get_barrier_semaphore()
-    for dy in steps_y:
-        for dx in steps_x:
-            for k in range(gz):
-                if (dy, dx, k) != (0, 0, 0):
-                    def greet(dy=dy, dx=dx, k=k):
-                        pl.semaphore_signal(
-                            barrier, inc=1, device_id=device(peer(k), dy, dx), device_id_type=MESH
-                        )
-                    when(exists(dy, dx), greet)
-    span_y = 1 + (at_y > 0).astype(jnp.int32) + (at_y < gy - 1).astype(jnp.int32)
-    span_x = 1 + (at_x > 0).astype(jnp.int32) + (at_x < gx - 1).astype(jnp.int32)
-    pl.semaphore_wait(barrier, gz * span_y * span_x - 1)
-
-    lanes = packed.shape[2]
+    wide = packed.shape[2]
     last = (by - 2) * slab // LANES * LANES
 
     def part(dy):
-        return {0: slice(0, lanes), 1: slice(last, last + LANES), -1: slice(0, LANES)}[dy]
+        return {0: slice(0, wide), 1: slice(last, last + LANES), -1: slice(0, LANES)}[dy]
 
     def clean_middle(dy, k):
         target = peer(k)
@@ -445,30 +467,7 @@
                     ).wait_recv()
                 when(exists(dy, dx), await_side)
 
-    for ok, make in late:
-        when(ok, lambda make=make: make().wait_send())
-
-
-def segment_kernel(
-    sizes,
-    where_ref,
-    m3,
-    x3,
-    narrow_ref,
-    wide_ref,
-    in_ref,
-    last_ref,
-    clean_ref,
-    out_ref,
-    middle_ref,
-    edge_ref,
-    taps,
-    result,
-):
-    gz, gy, gx = sizes
-    lines, planes, bx = middle_ref.shape
-    by, bz = lines - 4, planes - 4
-    me, at_y, at_x = where_ref[0], where_ref[1], where_ref[2]
+    lines, planes = by + 4, bz + 4
     slab = bx // gz
     lane = lane_of((bz + 4, LANES))
     for line in range(by + 4):
@@ -485,14 +484,8 @@
         after = pltpu.roll(x3[index, 1, :, lanes], (-off) % LANES, 1)
         edge_ref[line] = jnp.where(lane < LANES // 2, after, before)
 
-    in_left = left_rows(narrow_ref[96:144, :])
-    out_left = left_rows(
-        jnp.concatenate([wide_ref[48 * a + 32 : 48 * a + 48, :] for a in range(3)], axis=0)
-    )
-    in_bias = jnp.concatenate([column(in_ref)] * 3, axis=0)
-    out_bias = column(last_ref)
     for y in range(by + 2):
-        taps[y, pl.ds(15, planes, stride=16), :] = jnp.zeros((planes, bx), F32)
+        seg_taps[y, pl.ds(15, planes, stride=16), :] = jnp.zeros((planes, bx), F32)
     lane = lane_of((planes, bx))
     for line in range(lines):
         middle, edge = middle_ref[line], edge_ref[line]
@@ -504,7 +497,7 @@
                 value = pltpu.roll(jnp.where(lane < s - 2, edge, middle), bx - (s - 2), 1)
             for b in range(3):
                 if 0 <= line - b < by + 2:
-                    taps[line - b, pl.ds(b * 5 + s, planes, stride=16), :] = value
+                    seg_taps[line - b, pl.ds(b * 5 + s, planes, stride=16), :] = value
 
     for z in range(bz):
         clean_ref[z] = middle_ref[2 : 2 + by, 2 + z, :]
@@ -516,7 +509,7 @@
     mask = jnp.where(inside, 1.0, 0.0).astype(F32)
     partial = []
     for z in range(bz + 2):
-        rows = jnp.concatenate([taps[y, z * 16 : z * 16 + 48, :] for y in range(by + 2)], axis=1)
+        rows = jnp.concatenate([seg_taps[y, z * 16 : z * 16 + 48, :] for y in range(by + 2)], axis=1)
         high, low = split(rows)
         grown = jnp.maximum(mxu(in_left, right_rows(high, low)) + in_bias, 0.0) * mask
         if z == 0:
@@ -532,20 +525,10 @@
             for y in range(by):
                 result[pl.ds((z - 2) * by + y, 16, stride=bz * by), :] = total[:, y * bx : (y + 1) * bx]
     out_ref[...] = result[0 : 16 * bz * by, :]
-
-
-def narrow_rows(weight):
-    parts = weight.shape[0] // 16
-    kernel = weight.reshape(parts, 16, 3, 3, 3)
-    moved = jnp.stack(
-        [jnp.pad(kernel, ((0, 0),) * 4 + ((c, 2 - c),)) for c in range(3)], axis=1
-    ).reshape(parts * 48, 3, 15)
-    return jnp.pad(moved, ((0, 0), (0, 0), (0, 1))).reshape(parts * 48, 48)
-
-
-def wide_rows(weight):
-    outs, ins = weight.shape[0], weight.shape[1]
-    return weight.reshape(outs, ins, 3, 9).transpose(2, 0, 3, 1).reshape(3 * outs, 9 * ins)
+    for ok, make in sends:
+        when(ok, lambda make=make: make().wait_send())
+    for ok, make in late:
+        when(ok, lambda make=make: make().wait_send())
 
 
 def body(sizes, noisy, first_weight, first_bias, second_weight, second_bias, head_weight,
@@ -557,76 +540,69 @@
     tiles = -(-(by + 2) * slab // LANES)
     out_lanes = by * slab
     out_tiles = -(-out_lanes // LANES)
-    narrow = narrow_rows(jnp.concatenate([first_weight, seg_weight_in], axis=0))
-    wide = wide_rows(jnp.concatenate([second_weight, seg_weight_out], axis=0))
-    rows = [v.reshape(1, -1) for v in (first_bias, second_bias, head_weight, seg_bias_in, seg_bias_out)]
+    lanes = out_tiles * LANES
+    args = [
+        noisy.reshape(bz * by, bx),
+        first_weight.transpose(2, 1, 0),
+        first_bias.reshape(1, -1),
+        second_weight.transpose(2, 1, 0),
+        second_bias.reshape(1, -1),
+        head_weight.reshape(1, -1),
+        seg_weight_in,
+        seg_bias_in.reshape(1, -1),
+        seg_weight_out,
+        seg_bias_out.reshape(1, -1),
+    ]
     vmem = pl.BlockSpec(memory_space=pltpu.VMEM)
     dma = pltpu.SemaphoreType.DMA
-    smem = pl.BlockSpec(memory_space=pltpu.SMEM)
-    blocks = jax.ShapeDtypeStruct((gz, bz * by, bx), F32)
-    halos = jax.ShapeDtypeStruct((2, gz, bz * 2, bx), F32)
-    m1, x1, my, xy, where = pl.pallas_call(
-        functools.partial(gather_kernel, sizes, by),
-        out_shape=[blocks, blocks, halos, halos, jax.ShapeDtypeStruct((3,), jnp.int32)],
-        in_specs=[vmem],
-        out_specs=[vmem] * 4 + [smem],
-        scratch_shapes=[
-            pltpu.VMEM((2, bz * 2, bx), F32), dma((3, gz)), dma((3, gz)), dma((3, 2)), dma((3, gz))
-        ],
-        compiler_params=pltpu.CompilerParams(collective_id=0, has_side_effects=True),
-        name="gather",
-    )(noisy.reshape(bz * by, bx))
-    packed = pl.pallas_call(
-        functools.partial(layers_kernel, sizes, (bz, by, bx)),
-        out_shape=jax.ShapeDtypeStruct((gz, bz + 4, out_tiles * LANES), F32),
-        in_specs=[smem] + [vmem] * 9,
-        out_specs=vmem,
-        scratch_shapes=[
-            pltpu.VMEM((tiles, (depth + 2) * 16, LANES), F32),
-            pltpu.VMEM((tiles, (depth + 2) * 16, LANES), BF16),
-            pltpu.VMEM((tiles, (depth + 2) * 16, LANES), BF16),
-            pltpu.VMEM((depth + 2, 96, out_lanes), F32),
-            pltpu.VMEM((depth + 16, out_tiles * LANES), F32),
-        ],
-        name="layers",
-    )(
-        where,
-        m1.reshape(depth * by, bx),
-        x1.reshape(depth * by, bx),
-        my.reshape(2, depth * 2, bx),
-        xy.reshape(2, depth * 2, bx),
-        narrow,
-        wide,
-        *rows[:3],
-    )
-    m3, x3 = pl.pallas_call(
-        functools.partial(scatter_kernel, sizes, by, slab),
-        out_shape=[
-            jax.ShapeDtypeStruct((3, gz, bz + 4, out_tiles * LANES), F32),
-            jax.ShapeDtypeStruct((3, 2, bz + 4, out_tiles * LANES), F32),
-        ],
-        in_specs=[vmem],
-        out_specs=[vmem] * 2,
-        scratch_shapes=[dma((3, gz)), dma((3, gz)), dma((3, 2, gz)), dma((3, 2))],
-        compiler_params=pltpu.CompilerParams(collective_id=1, has_side_effects=True),
-        name="scatter",
-    )(packed)
+    rest = pl.BlockSpec(memory_space=pl.ANY)
+
+    def room(*shape):
+        return pltpu.VMEM(shape, F32)
+
+    stages = [
+        room(*(a.shape if i not in (1, 6) else (a.shape[0], a.shape[2]))) for i, a in enumerate(args)
+    ]
     clean, features = pl.pallas_call(
-        functools.partial(segment_kernel, sizes),
+        functools.partial(whole_kernel, sizes, bz, by, bx),
         out_shape=[
             jax.ShapeDtypeStruct((bz, by, bx), F32),
             jax.ShapeDtypeStruct((16 * bz * by, bx), F32),
         ],
-        in_specs=[smem] + [vmem] * 6,
+        in_specs=[rest] * len(args),
         out_specs=[vmem] * 2,
-        scratch_shapes=[
-            pltpu.VMEM((by + 4, bz + 4, bx), F32),
-            pltpu.VMEM((by + 4, bz + 4, bx), F32),
-            pltpu.VMEM((by + 2, (bz + 5) * 16, bx), F32),
-            pltpu.VMEM((17 * bz * by, bx), F32),
+        scratch_shapes=stages
+        + [
+            dma((len(args),)),
+            room(depth * by, bx),
+            room(depth * by, bx),
+            room(2, depth * 2, bx),
+            room(2, depth * 2, bx),
+            room(2, bz * 2, bx),
+            dma((3, gz)),
+            dma((3, gz)),
+            dma((3, 2)),
+            dma((3, gz)),
+            room(tiles, (depth + 2) * 16, LANES),
+            pltpu.VMEM((tiles, (depth + 2) * 16, LANES), BF16),
+            pltpu.VMEM((tiles, (depth + 2) * 16, LANES), BF16),
+            room(depth + 2, 96, out_lanes),
+            room(depth + 16, lanes),
+            room(gz, bz + 4, lanes),
+            room(3, gz, bz + 4, lanes),
+            room(3, 2, bz + 4, lanes),
+            dma((3, gz)),
+            dma((3, gz)),
+            dma((3, 2, gz)),
+            dma((3, 2)),
+            room(by + 4, bz + 4, bx),
+            room(by + 4, bz + 4, bx),
+            room(by + 2, (bz + 5) * 16, bx),
+            room(17 * bz * by, bx),
         ],
-        name="segment",
-    )(where, m3, x3, narrow, wide, *rows[3:])
+        compiler_params=pltpu.CompilerParams(collective_id=0, has_side_effects=True),
+        name="whole",
+    )(*args)
     return clean, features.reshape(16, bz, by, bx)
 
 

time: 32.9 us -> 25 us (0.76)
  Pallas kernels: 28.1 us -> 21 us
  other arithmetic: 0.49 us -> 0 us
    pallas_call x4 -> x1, Pallas kernels: 28.1 us -> 21 us  [body(): pl.pallas_call(functools.partial(whole_kernel, sizes, bz, by, bx), out_sh...]
    reshape x6 -> x0, local copies, waits for them, and re-layouts: 2.01 us -> none  [the longest x3 1.03 us: wide_rows(): weight.reshape(outs, ins, 3, 9).transpose(2, 0, 3, 1)]
    unnamed x8 -> x2, local copies, waits for them, and re-layouts: 0.99 us -> 2.99 us
where the time goes in v1:
time: 25 us; the launch traced here: 24.6 us
  Pallas kernels  21 us (84%)
  local copies, waits for them, and re-layouts  2.99 us (12%)
  between operations  0.64 us (3%)
    pallas_call x1, Pallas kernels, body(): pl.pallas_call(functools.partial(whole_kernel, sizes, bz, by, bx), out_sh...  21 us
    unnamed x2, local copies, waits for them, and re-layouts  2.99 us

profile of v1, /device:TPU:0, one launch (start us, length us, event | category | flops | bytes accessed | tf_op | source)
XLA Modules:
  0.0 24.6 jit_solution(3610017180064114668)
XLA Ops:
  0.6 21.0 %whole.1 = (f32[4,8,128]{2,1,0:T(8,128)}, f32[512,128]{1,0:T(8,128)}) custom-call(f32[32,128]{1,0:T(8,128)} %bitcast.11, f32[27,1,32]{2,1,0:T(1,128)} %bitcast.12, f32[1,16]{1,0:T(1,128)} %bitcast.13, f32[27,16,32]{2,1,0:T(8,128)} %bitcast.10, f32[1,16]{1,0:T(1,128)} %bitcast.14, f32[1,16]{1,0:T(1,128)} %bitcast.15, f32[16,1,27]{2,1,0:T(1,128)} %w3_any.1, ...), custom_call_target="tpu_custom_call" | custom-call | tf_op jit(solution)/shard_map/whole/pallas_call | solution.py:566
  21.6 1.3 %copy.14 = f32[4,8,128]{2,1,0:T(8,128)} copy(f32[4,8,128]{2,1,0:T(8,128)} %get-tuple-element.8) | data formatting | bytes 32768
  23.0 1.7 %copy.15 = f32[16,4,8,128]{3,2,1,0:T(8,128)} copy(f32[16,4,8,128]{3,2,1,0:T(8,128)} %bitcast.9) | data formatting | bytes 524288

commit v2 on v1

--- a/solution.py
+++ b/solution.py
@@ -8,6 +8,7 @@
 from jax.sharding import PartitionSpec as P
 
 LANES = 128
+GRANT = 40 << 20
 F32 = jnp.float32
 BF16 = jnp.bfloat16
 MESH = pl.DeviceIdType.MESH
@@ -112,15 +113,14 @@
     return jnp.concatenate([high, high, low], axis=1)
 
 
-def whole_kernel(
+def layers_kernel(
     sizes, bz, by, bx,
     noisy_any, w1_any, b1_any, w2_any, b2_any, head_any, w3_any, b3_any, w4_any, b4_any,
-    clean_ref, out_ref,
+    middle_ref, edge_ref, in_left_ref, out_left_ref, in_bias_ref, out_bias_ref,
     noisy_ref, w1_ref, b1_ref, w2_ref, b2_ref, head_ref, w3_ref, b3_ref, w4_ref, b4_ref, load_sem,
     m1, x1, my, xy, halo, m1_send, m1_recv, x1_send, x1_recv,
     wide_taps, taps_high, taps_low, product, fix, packed,
     m3, x3, m3_send, m3_recv, x3_send, x3_recv,
-    middle_ref, edge_ref, seg_taps, result,
 ):
     gz, gy, gx = sizes
     depth = gz * bz
@@ -265,10 +265,12 @@
     turned = w1_ref[...].T
     first_left = narrow_left(turned)
     second_left = wide_left(w2_ref[...].reshape(-1, w2_ref.shape[2]))
-    in_left = narrow_left(w3_ref[...])
-    out_left = last_left(w4_ref[...])
-    in_bias = jnp.concatenate([column(b3_ref)] * 3, axis=0)
-    out_bias = column(b4_ref)
+    in_left_ref[...] = narrow_left(w3_ref[...])
+    out_left_ref[...] = last_left(w4_ref[...])
+    in_bias_ref[...] = jnp.broadcast_to(
+        jnp.concatenate([column(b3_ref)] * 3, axis=0), in_bias_ref.shape
+    )
+    out_bias_ref[...] = jnp.broadcast_to(column(b4_ref), out_bias_ref.shape)
     first_bias = jnp.concatenate([column(b1_ref)] * 3, axis=0)
     second_bias = column(b2_ref)
     head = column(head_ref)
@@ -483,7 +485,26 @@
         before = pltpu.roll(x3[index, 0, :, lanes], (bx - off - slab) % LANES, 1)
         after = pltpu.roll(x3[index, 1, :, lanes], (-off) % LANES, 1)
         edge_ref[line] = jnp.where(lane < LANES // 2, after, before)
-
+    for ok, make in sends:
+        when(ok, lambda make=make: make().wait_send())
+    for ok, make in late:
+        when(ok, lambda make=make: make().wait_send())
+
+
+def segment_kernel(
+    sizes, middle_ref, edge_ref, in_left_ref, out_left_ref, in_bias_ref, out_bias_ref,
+    clean_ref, out_ref, seg_taps, result,
+):
+    gz, gy, gx = sizes
+    lines, planes, bx = middle_ref.shape
+    by, bz = lines - 4, planes - 4
+    me = lax.axis_index("gz")
+    at_y = lax.axis_index("gy")
+    at_x = lax.axis_index("gx")
+    in_left = in_left_ref[...]
+    out_left = out_left_ref[...]
+    in_bias = in_bias_ref[:, 0:1]
+    out_bias = out_bias_ref[:, 0:1]
     for y in range(by + 2):
         seg_taps[y, pl.ds(15, planes, stride=16), :] = jnp.zeros((planes, bx), F32)
     lane = lane_of((planes, bx))
@@ -525,11 +546,6 @@
             for y in range(by):
                 result[pl.ds((z - 2) * by + y, 16, stride=bz * by), :] = total[:, y * bx : (y + 1) * bx]
     out_ref[...] = result[0 : 16 * bz * by, :]
-    for ok, make in sends:
-        when(ok, lambda make=make: make().wait_send())
-    for ok, make in late:
-        when(ok, lambda make=make: make().wait_send())
-
 
 def body(sizes, noisy, first_weight, first_bias, second_weight, second_bias, head_weight,
          seg_weight_in, seg_bias_in, seg_weight_out, seg_bias_out):
@@ -563,14 +579,18 @@
     stages = [
         room(*(a.shape if i not in (1, 6) else (a.shape[0], a.shape[2]))) for i, a in enumerate(args)
     ]
-    clean, features = pl.pallas_call(
-        functools.partial(whole_kernel, sizes, bz, by, bx),
+    handed = pl.pallas_call(
+        functools.partial(layers_kernel, sizes, bz, by, bx),
         out_shape=[
-            jax.ShapeDtypeStruct((bz, by, bx), F32),
-            jax.ShapeDtypeStruct((16 * bz * by, bx), F32),
+            room(by + 4, bz + 4, bx),
+            room(by + 4, bz + 4, bx),
+            pltpu.VMEM((48, 144), BF16),
+            pltpu.VMEM((48, 432), BF16),
+            room(48, LANES),
+            room(16, LANES),
         ],
         in_specs=[rest] * len(args),
-        out_specs=[vmem] * 2,
+        out_specs=[vmem] * 6,
         scratch_shapes=stages
         + [
             dma((len(args),)),
@@ -595,14 +615,24 @@
             dma((3, gz)),
             dma((3, 2, gz)),
             dma((3, 2)),
-            room(by + 4, bz + 4, bx),
-            room(by + 4, bz + 4, bx),
-            room(by + 2, (bz + 5) * 16, bx),
-            room(17 * bz * by, bx),
         ],
-        compiler_params=pltpu.CompilerParams(collective_id=0, has_side_effects=True),
-        name="whole",
-    )(*args)
+        compiler_params=pltpu.CompilerParams(
+            collective_id=0, has_side_effects=True, vmem_limit_bytes=GRANT
+        ),
+        name="layers",
+    )(*(pltpu.with_memory_space_constraint(a, pltpu.HBM) for a in args))
+    clean, features = pl.pallas_call(
+        functools.partial(segment_kernel, sizes),
+        out_shape=[
+            jax.ShapeDtypeStruct((bz, by, bx), F32),
+            jax.ShapeDtypeStruct((16 * bz * by, bx), F32),
+        ],
+        in_specs=[vmem] * 6,
+        out_specs=[vmem] * 2,
+        scratch_shapes=[room(by + 2, (bz + 5) * 16, bx), room(17 * bz * by, bx)],
+        compiler_params=pltpu.CompilerParams(vmem_limit_bytes=GRANT),
+        name="segment",
+    )(*handed)
     return clean, features.reshape(16, bz, by, bx)
 
 

time: 25 us -> 22.1 us (0.88)
  local copies, waits for them, and re-layouts: 2.99 us -> 0 us
    unnamed x2 -> x0, local copies, waits for them, and re-layouts: 2.99 us -> none
    pallas_call x1 -> x2, Pallas kernels: 21 us -> 21.2 us  [the longest x1 18.3 us: body(): pl.pallas_call(functools.partial(layers_kernel, sizes, bz, by, bx), out_s...]
where the time goes in v2:
time: 22.1 us; the launch traced here: 21.8 us
  Pallas kernels  21.2 us (96%)
  between operations  0.64 us (3%)
    pallas_call x1, Pallas kernels, body(): pl.pallas_call(functools.partial(layers_kernel, sizes, bz, by, bx), out_s...  18.3 us
    pallas_call x1, Pallas kernels, body(): pl.pallas_call(functools.partial(segment_kernel, sizes), out_shape=[jax.S...  2.83 us

profile of v2, /device:TPU:0, one launch (start us, length us, event | category | flops | bytes accessed | tf_op | source)
XLA Modules:
  0.0 21.8 jit_solution(16540139220747643082)
XLA Ops:
  0.6 18.3 %layers.1 = (f32[12,8,128]{2,1,0:T(8,128)S(1)}, f32[12,8,128]{2,1,0:T(8,128)S(1)}, bf16[48,144]{1,0:T(8,128)(2,1)S(1)}, bf16[48,432]{1,0:T(8,128)(2,1)S(1)}, f32...) custom-call(f32[32,128]{1,0:T(8,128)} %bitcast.10, f32[27,1,32]{2,1,0:T(1,128)} %bitcast.11, f32[1,16]{1,0:T(1,128)} %bitcast.12, ...), custom_call_target="tpu_custom_call" | custom-call | tf_op jit(solution)/shard_map/layers/pallas_call | solution.py:582
  19.0 2.8 %segment.1 = (f32[4,8,128]{2,1,0:T(8,128)}, f32[512,128]{1,0:T(8,128)}) custom-call(f32[12,8,128]{2,1,0:T(8,128)S(1)} %get-tuple-element.10.middle_ref, f32[12,8,128]{2,1,0:T(8,128)S(1)} %get-tuple-element.11.edge_ref, bf16[48,144]{1,0:T(8,128)(2,1)S(1)} %get-tuple-element.12.in_left_ref, bf16[48,432]{1,0:T(8,128)(2,1)S(1)} %get-tuple-element.13.out_left_ref, ...), custom_call_target="tpu_custom_call" | custom-call | tf_op jit(solution)/shard_map/segment/pallas_call | solution.py:624

commit v3 on v2

v3 whole, which is shorter than its diff:
```python
import functools

import jax
import jax.numpy as jnp
from jax import lax
from jax.experimental import pallas as pl
from jax.experimental.pallas import tpu as pltpu
from jax.sharding import PartitionSpec as P

LANES = 128
GRANT = 40 << 20
F32 = jnp.float32
BF16 = jnp.bfloat16
MESH = pl.DeviceIdType.MESH


def split(value):
    high = value.astype(BF16)
    return high, (value - high.astype(F32)).astype(BF16)


def left_rows(weight):
    high, low = split(weight)
    return jnp.concatenate([high, high, low], axis=1)


def right_rows(high, low):
    return jnp.concatenate([high, low, high], axis=0)


def mxu(left, right):
    return jnp.dot(left, right, preferred_element_type=F32)


def lane_of(shape):
    return lax.broadcasted_iota(jnp.int32, shape, len(shape) - 1)


def row_of(shape):
    return lax.broadcasted_iota(jnp.int32, shape, 0)


def column(row_ref):
    count = row_ref.shape[1]
    shape = (count, count)
    spread = jnp.broadcast_to(row_ref[...], shape)
    return jnp.sum(jnp.where(row_of(shape) == lane_of(shape), spread, 0.0), axis=1, keepdims=True)


def times(count, step, carry, backward=False):
    if count <= 16:
        for i in range(count):
            carry = step(count - 1 - i if backward else i, carry)
        return carry
    return lax.fori_loop(0, count, lambda i, c: step(count - 1 - i if backward else i, c), carry)


def aligned(start, unit):
    return start if isinstance(start, int) else pl.multiple_of(start, unit)


def matches(left, right):
    return jnp.where(left == right, 1.0, 0.0).astype(BF16)


def spread_narrow(weight, shift):
    taps = weight.shape[1]
    shape = (taps, 48)
    tap, col = row_of(shape), lane_of(shape)
    plane = (tap >= 9).astype(jnp.int32) + (tap >= 18).astype(jnp.int32)
    rest = tap - 9 * plane
    line = (rest >= 3).astype(jnp.int32) + (rest >= 6).astype(jnp.int32)
    place = matches(col, tap + 7 * plane + 2 * line + shift)
    return tuple(mxu(part, place).astype(BF16) for part in split(weight))


def narrow_left(weight):
    parts = weight.shape[0] // 16
    highs, lows = [], []
    for part in range(parts):
        for shift in range(3):
            high, low = spread_narrow(weight[16 * part : 16 * part + 16], shift)
            highs.append(high)
            lows.append(low)
    high, low = jnp.concatenate(highs, axis=0), jnp.concatenate(lows, axis=0)
    return jnp.concatenate([high, high, low], axis=1)


def first_rows(weight, bias, lines):
    taps = weight.shape[1]
    block = 10 * (lines + 4)
    shape = (taps, 3 * block)
    tap, col = row_of(shape), lane_of(shape)
    plane = (tap >= 9).astype(jnp.int32) + (tap >= 18).astype(jnp.int32)
    rest = tap - 9 * plane
    line = (rest >= 3).astype(jnp.int32) + (rest >= 6).astype(jnp.int32)
    start = (lines + 4) * (3 * (rest - 3 * line) + plane) + line
    high, low = split(weight)
    half = weight.shape[0] // 2
    shape = (half, 3 * block)
    steady = jnp.zeros(shape, F32)
    for piece in range(3):
        piece_of = bias.astype(BF16).astype(F32)
        steady = jnp.where(lane_of(shape) == 9 * (lines + 4) + piece, piece_of, steady)
        bias = bias - piece_of
    steady = jnp.concatenate([jnp.zeros(shape, F32), steady], axis=0)
    parts = []
    for at in range(lines + 2):
        first = matches(col, start + at) + matches(col, start + at + block)
        last = matches(col, start + at + 2 * block)
        parts.append((mxu(high, first) + mxu(low, last) + steady).astype(BF16))
    return jnp.concatenate([p[:half] for p in parts] + [p[half:] for p in parts], axis=0)


def second_rows(turned, ins):
    return left_rows(
        jnp.concatenate(
            [
                jnp.concatenate(
                    [
                        turned[ins * (9 * a + 3 * b + c) : ins * (9 * a + 3 * b + c + 1)]
                        for c in range(3)
                        for b in range(3)
                    ],
                    axis=0,
                ).T
                for a in range(3)
            ],
            axis=0,
        )
    )


def last_left(weight):
    outs, ins, taps = weight.shape
    shape = (taps, taps * ins)
    place = matches(row_of(shape), lane_of(shape) // ins)
    shape = (outs * ins, taps * ins)
    keep = (row_of(shape) % ins) == (lane_of(shape) % ins)
    shape = (outs, outs * ins)
    gather = matches(row_of(shape), lane_of(shape) // ins)
    parts = []
    for part in split(weight.reshape(outs * ins, taps)):
        grown = jnp.where(keep, mxu(part, place), 0.0).astype(BF16)
        parts.append(mxu(gather, grown).astype(BF16))
    third = taps * ins // 3
    high, low = (
        jnp.concatenate([p[:, third * a : third * (a + 1)] for a in range(3)], axis=0) for p in parts
    )
    return jnp.concatenate([high, high, low], axis=1)


def layers_kernel(
    sizes, ranks, bz, by, bx,
    noisy_any, w1_any, b1_any, w2_any, b2_any, head_any, w3_any, b3_any, w4_any, b4_any,
    own_ref, beside_ref, edge_ref, in_left_ref, out_left_ref, in_bias_ref, out_bias_ref,
    noisy_ref, w1_ref, b1_ref, w2_ref, b2_ref, head_ref, w3_ref, b3_ref, w4_ref, b4_ref, load_sem,
    m1, my, x1, halo, rim, send1, recv1,
    shifted, ready, product, fix, packed, packed_rim,
    x3, own_send, own_recv, beside_send, beside_recv, edge_send, corner_send, edge_recv,
):
    gz, gy, gx = sizes
    depth = gz * bz
    part = by // ranks
    lines = part + 4
    rows = part + 2
    me = lax.axis_index("gz")
    at_y = lax.axis_index("gy")
    at_x = lax.axis_index("gx")
    works = me < ranks
    steps_y = (-1, 1) if gy > 1 else ()
    steps_x = (-1, 1) if gx > 1 else ()

    def exists(dy, dx):
        ok = None
        for where, step, count in ((at_y, dy, gy), (at_x, dx, gx)):
            if step == 0:
                continue
            here = where > 0 if step < 0 else where < count - 1
            ok = here if ok is None else ok & here
        return ok

    def both(first, second):
        return second if first is None else first if second is None else first & second

    def when(ok, action):
        if ok is None:
            action()
        else:
            pl.when(ok)(action)

    def device(z, dy, dx):
        return {
            "win": lax.axis_index("win"),
            "gz": z,
            "gy": lax.rem(at_y + dy + gy, gy),
            "gx": lax.rem(at_x + dx + gx, gx),
        }

    def peer(k):
        return lax.rem(me + k, gz)

    def rank_towards(dy):
        return 0 if dy > 0 else ranks - 1

    def side(step):
        return (step + 1) // 2

    loads = [
        pltpu.make_async_copy(source, target, load_sem.at[i])
        for i, (source, target) in enumerate(
            (
                (noisy_any, noisy_ref),
                (w1_any.at[:, 0, :], w1_ref),
                (w2_any, w2_ref),
                (w3_any.at[:, 0, :], w3_ref),
                (w4_any, w4_ref),
                (b1_any, b1_ref),
                (b2_any, b2_ref),
                (head_any, head_ref),
                (b3_any, b3_ref),
                (b4_any, b4_ref),
            )
        )
    ]
    loads[0].start()
    barrier = pltpu.get_barrier_semaphore()

    def greet(dy, dx):
        for k in range(gz - 1, -1, -1):
            if (dy, dx, k) != (0, 0, 0):
                pl.semaphore_signal(barrier, inc=1, device_id=device(peer(k), dy, dx), device_id_type=MESH)

    for dx in (0,) + steps_x:
        when(both(works, exists(0, dx)), functools.partial(greet, 0, dx))
    for dy in steps_y:
        for dx in (0,) + steps_x:
            when(both(me == rank_towards(-dy), exists(dy, dx)), functools.partial(greet, dy, dx))
    for load in loads[1:]:
        load.start()

    loads[0].wait()
    for index, first in ((0, 0), (1, by - 2)):
        for z in range(bz):
            halo[index, 2 * z : 2 * z + 2, :] = noisy_ref[z * by + first : z * by + first + 2, :]
    lane = lane_of((by, bx))
    corner = jnp.zeros((by, bx), F32)
    for z in range(bz):
        turned = pltpu.roll(noisy_ref[z * by : (z + 1) * by, :], 4 * z + 2, 1)
        corner = jnp.where((lane >= 4 * z) & (lane < 4 * z + 4), turned, corner)
    rim[...] = corner

    count_y = (at_y > 0).astype(jnp.int32) + (at_y < gy - 1).astype(jnp.int32)
    count_x = (at_x > 0).astype(jnp.int32) + (at_x < gx - 1).astype(jnp.int32)
    pl.semaphore_wait(
        barrier, ranks - works.astype(jnp.int32) + count_y + count_x * ranks + count_y * count_x
    )

    def rows_of(z, count):
        return pl.ds(aligned(z * count, count), count)

    def own_first(k, source):
        return pltpu.make_async_remote_copy(
            src_ref=noisy_ref,
            dst_ref=m1.at[rows_of(source, bz * by), :],
            send_sem=send1.at[0, k],
            recv_sem=recv1.at[0, source],
            device_id=device(k, 0, 0),
            device_id_type=MESH,
        )

    def halo_first(dy, source):
        return pltpu.make_async_remote_copy(
            src_ref=halo.at[side(dy)],
            dst_ref=my.at[side(-dy), rows_of(source, bz * 2), :],
            send_sem=send1.at[1, side(dy)],
            recv_sem=recv1.at[1 + side(-dy), source],
            device_id=device(rank_towards(dy), dy, 0),
            device_id_type=MESH,
        )

    def edge_first(dx, k, source):
        return pltpu.make_async_remote_copy(
            src_ref=rim,
            dst_ref=x1.at[0, side(-dx), source],
            send_sem=send1.at[2 + side(dx), k],
            recv_sem=recv1.at[3 + side(-dx), source],
            device_id=device(k, 0, dx),
            device_id_type=MESH,
        )

    def corner_first(dy, dx, source):
        return pltpu.make_async_remote_copy(
            src_ref=rim,
            dst_ref=x1.at[1 + side(-dy), side(-dx), source],
            send_sem=send1.at[4 + side(dy), side(dx)],
            recv_sem=recv1.at[5 + 2 * side(-dy) + side(-dx), source],
            device_id=device(rank_towards(dy), dy, dx),
            device_id_type=MESH,
        )

    early = []
    for dy in steps_y:
        early.append((exists(dy, 0), functools.partial(halo_first, dy)))
        for dx in steps_x:
            early.append((exists(dy, dx), functools.partial(corner_first, dy, dx)))
    for k in range(ranks):
        early.append((me != k, functools.partial(own_first, k)))
        for dx in steps_x:
            early.append((exists(0, dx), functools.partial(edge_first, dx, k)))
    for ok, make in early:
        when(ok, lambda make=make: make(me).start())

    for load in loads[1:]:
        load.wait()
    for index, ok in ((0, at_y == 0), (1, at_y == gy - 1)):
        def no_row(index=index):
            my[index] = jnp.zeros(my.shape[1:], F32)
            x1[1 + index] = jnp.zeros(x1.shape[1:], F32)
            beside_ref[index] = jnp.zeros(beside_ref.shape[1:], F32)
            x3[ranks + index] = jnp.zeros(x3.shape[1:], F32)
        pl.when(ok)(no_row)
    for index, ok in ((0, at_x == 0), (1, at_x == gx - 1)):
        def no_side(index=index):
            for slot in range(3):
                x1[slot, index] = jnp.zeros(x1.shape[2:], F32)
            for slot in range(ranks + 2):
                x3[slot, index] = jnp.zeros(x3.shape[2:], F32)
        pl.when(ok)(no_side)
    in_left_ref[...] = narrow_left(w3_ref[...])
    out_left_ref[...] = last_left(w4_ref[...])
    in_bias_ref[...] = jnp.broadcast_to(jnp.concatenate([column(b3_ref)] * 3, axis=0), in_bias_ref.shape)
    out_bias_ref[...] = jnp.broadcast_to(column(b4_ref), out_bias_ref.shape)

    def own_last(k, target):
        return pltpu.make_async_remote_copy(
            src_ref=packed.at[target],
            dst_ref=own_ref.at[k],
            send_sem=own_send.at[target],
            recv_sem=own_recv.at[k],
            device_id=device(target, 0, 0),
            device_id_type=MESH,
        )

    def halo_last(dy, target):
        start = 0 if dy < 0 else (part - 2) * bx
        return pltpu.make_async_remote_copy(
            src_ref=packed.at[target, :, start : start + 2 * bx],
            dst_ref=beside_ref.at[side(-dy)],
            send_sem=beside_send.at[side(dy), target],
            recv_sem=beside_recv.at[side(-dy)],
            device_id=device(target, dy, 0),
            device_id_type=MESH,
        )

    def edge_last(dx, k, target):
        return pltpu.make_async_remote_copy(
            src_ref=packed_rim.at[target],
            dst_ref=x3.at[k, side(-dx)],
            send_sem=edge_send.at[side(dx), target],
            recv_sem=edge_recv.at[k, side(-dx)],
            device_id=device(target, 0, dx),
            device_id_type=MESH,
        )

    def corner_last(dy, dx, target):
        return pltpu.make_async_remote_copy(
            src_ref=packed_rim.at[target],
            dst_ref=x3.at[ranks + side(-dy), side(-dx)],
            send_sem=corner_send.at[side(dy), side(dx), target],
            recv_sem=edge_recv.at[ranks + side(-dy), side(-dx)],
            device_id=device(target, dy, dx),
            device_id_type=MESH,
        )

    late = []
    for target in range(gz):
        late.append((me != target, functools.partial(own_last, me, target)))
        for dy in steps_y:
            ok = both(me == rank_towards(-dy), exists(dy, 0))
            late.append((ok, functools.partial(halo_last, dy, target)))
        for dx in steps_x:
            late.append((exists(0, dx), functools.partial(edge_last, dx, me, target)))
        for dy in steps_y:
            for dx in steps_x:
                ok = both(me == rank_towards(-dy), exists(dy, dx))
                late.append((ok, functools.partial(corner_last, dy, dx, target)))

    @pl.when(works)
    def layers():
        first_left = first_rows(w1_ref[...].T, column(b1_ref), part)
        second_left = second_rows(w2_ref[...].reshape(-1, w2_ref.shape[2]), w2_ref.shape[1])
        second_bias = column(b2_ref)
        head = column(head_ref)
        shape = (16 * rows, 2 * bx)
        lane, row = lane_of(shape), row_of(shape)
        place_y = at_y * by + me * part + row // 16 - 1
        outside = (place_y < 0) | (place_y >= gy * by)
        outside = outside | ((at_x == 0) & (lane == 2 * bx - 1)) | ((at_x == gx - 1) & (lane == bx))
        mask = jnp.where(outside, 0.0, 1.0).astype(F32)
        for s in range(6):
            for plane in (0, depth + 1):
                shifted[s, plane * lines : (plane + 1) * lines, :] = jnp.zeros((lines, bx), F32)
        for plane in (0, depth + 1):
            product[plane] = jnp.zeros(product.shape[1:], F32)
        fix[...] = jnp.zeros(fix.shape, F32)
        m1[rows_of(me, bz * by), :] = noisy_ref[...]

        for k in range(1, gz):
            own_first(0, peer(k)).wait_recv()
        for dx in steps_x:
            def await_edges(dx=dx):
                for source in range(gz):
                    edge_first(-dx, 0, source).wait_recv()
            when(exists(0, dx), await_edges)
        for dy in steps_y:
            def await_halos(dy=dy):
                for source in range(gz):
                    halo_first(-dy, source).wait_recv()
            when(both(me == rank_towards(-dy), exists(dy, 0)), await_halos)
            for dx in steps_x:
                def await_corners(dy=dy, dx=dx):
                    for source in range(gz):
                        corner_first(-dy, -dx, source).wait_recv()
                when(both(me == rank_towards(-dy), exists(dy, dx)), await_corners)

        lane = lane_of((lines, bx))
        place = lane_of((by, bx)) % 4

        def mine(full):
            value = full[0:lines]
            for k in range(1, ranks):
                value = jnp.where(me == k, full[part * k : part * k + lines], value)
            return value

        def gather(m, carry):
            rims = [jnp.where(place < 2, x1[slot, 0, m], x1[slot, 1, m]) for slot in range(3)]
            border = mine(jnp.concatenate([rims[1][by - 2 : by], rims[0], rims[2][0:2]], axis=0))
            below = my[0, rows_of(m, bz * 2), :]
            above = my[1, rows_of(m, bz * 2), :]
            block = m1[rows_of(m, bz * by), :]
            for z in range(bz):
                value = mine(
                    jnp.concatenate(
                        [below[2 * z : 2 * z + 2], block[z * by : (z + 1) * by], above[2 * z : 2 * z + 2]],
                        axis=0,
                    )
                )
                beyond = pltpu.roll(border, (bx - 2 - 4 * z) % bx, 1)
                where = pl.ds(aligned((m * bz + z + 1) * lines, lines), lines)
                shifted[0, where, :] = pltpu.roll(jnp.where(lane == bx - 1, beyond, value), 1, 1)
                shifted[1, where, :] = value
                shifted[2, where, :] = pltpu.roll(jnp.where(lane == 0, beyond, value), bx - 1, 1)
                shifted[3, where, :] = pltpu.roll(jnp.where(lane == bx - 2, beyond, value), 1, 1)
                shifted[4, where, :] = beyond
                shifted[5, where, :] = pltpu.roll(jnp.where(lane == 1, beyond, value), bx - 1, 1)
            return carry

        times(gz, gather, 0)
        lane = lane_of((16 * rows, bx))
        spare = jnp.ones((lines, bx), F32)

        def gates(z, slot):
            window = pl.ds(aligned(z * lines, lines), 3 * lines)
            halves = [
                jnp.concatenate([shifted[s, window, :] for s in three] + [spare], axis=0)
                for three in (range(3), range(3, 6))
            ]
            high, low = split(jnp.concatenate(halves, axis=1))
            pre = mxu(first_left, right_rows(high, low))
            ready[0, slot] = mask * jnp.tanh(pre[0 : 16 * rows])
            ready[1, slot] = jax.nn.sigmoid(pre[16 * rows :])

        def advance(z, slot, hidden):
            hidden = hidden + ready[1, slot] * (ready[0, slot] - hidden)
            inner, outer = hidden[:, 0:bx], hidden[:, bx:]
            fields = (
                pltpu.roll(jnp.where(lane == bx - 1, outer, inner), 1, 1),
                inner,
                pltpu.roll(jnp.where(lane == 0, outer, inner), bx - 1, 1),
            )
            highs, lows = zip(*(split(f) for f in fields))

            def stacked(values):
                return jnp.concatenate(
                    [
                        jnp.concatenate([v[16 * j : 16 * j + 48] for j in range(part)], axis=1)
                        for v in values
                    ],
                    axis=0,
                )

            product[z + 1] = mxu(second_left, right_rows(stacked(highs), stacked(lows)))
            return hidden

        chunk = ready.shape[1]

        def forward(step, hidden):
            ahead = 16
            for slot in range(min(ahead, chunk)):
                gates(step * chunk + slot, slot)
            for slot in range(chunk):
                if slot + ahead < chunk:
                    gates(step * chunk + slot + ahead, slot + ahead)
                hidden = advance(step * chunk + slot, slot, hidden)
            return hidden

        times(depth // chunk, forward, jnp.zeros((16 * rows, 2 * bx), F32))

        def back(z, hidden):
            pre = product[z, 0:32] + product[z + 1, 32:64] + product[z + 2, 64:96]
            cand = jnp.tanh(pre[0:16])
            change = jax.nn.sigmoid(pre[16:32] + second_bias)
            hidden = hidden + change * (cand - hidden)
            fix[pl.ds(z + 2, 1), :] = jnp.sum(head * hidden, axis=0, keepdims=True)
            return hidden

        times(depth, back, jnp.zeros((16, part * bx), F32), True)
        lane = lane_of((fix.shape[0], bx))
        border = jnp.zeros((fix.shape[0], bx), F32)
        for j in range(part):
            lanes = slice(j * bx, (j + 1) * bx)
            centre = shifted[1, pl.ds(lines + j + 2, depth, stride=lines), :]
            fix[2 : 2 + depth, lanes] = fix[2 : 2 + depth, lanes] + centre
            turned = pltpu.roll(fix[:, lanes], 4 * j + 2, 1)
            border = jnp.where((lane >= 4 * j) & (lane < 4 * j + 4), turned, border)
        for target in range(gz):
            packed[target] = fix[bz * target : bz * target + bz + 4, :]
            packed_rim[target] = border[bz * target : bz * target + bz + 4]
        for ok, make in late:
            when(ok, lambda make=make: make().start())
        for k in range(ranks):
            def keep(k=k):
                own_ref[k] = packed[k]
            pl.when(me == k)(keep)

    for k in range(ranks):
        def await_own(k=k):
            own_last(k, 0).wait_recv()
        pl.when(me != k)(await_own)
    for dy in steps_y:
        def await_beside(dy=dy):
            halo_last(-dy, 0).wait_recv()
        when(exists(dy, 0), await_beside)
    for dx in steps_x:
        def await_rims(dx=dx):
            for k in range(ranks):
                edge_last(-dx, k, 0).wait_recv()
        when(exists(0, dx), await_rims)
        for dy in steps_y:
            def await_corner(dy=dy, dx=dx):
                corner_last(-dy, -dx, 0).wait_recv()
            when(exists(dy, dx), await_corner)
    place = lane_of((bz + 4, bx)) % 4
    for line in range(by + 4):
        if line < 2:
            slot, j = ranks, part - 2 + line
        elif line < by + 2:
            slot, j = (line - 2) // part, (line - 2) % part
        else:
            slot, j = ranks + 1, line - by - 2
        beyond = jnp.where(place < 2, x3[slot, 0], x3[slot, 1])
        edge_ref[line] = pltpu.roll(beyond, (bx - 2 - 4 * j) % bx, 1)
    for ok, make in early:
        when(ok, lambda make=make: make(me).wait_send())

    @pl.when(works)
    def drain():
        for ok, make in late:
            when(ok, lambda make=make: make().wait_send())


def segment_kernel(
    sizes, own_ref, beside_ref, edge_ref, in_left_ref, out_left_ref, in_bias_ref, out_bias_ref,
    clean_ref, out_ref, seg_taps, result,
):
    gz, gy, gx = sizes
    ranks = own_ref.shape[0]
    lines, planes, bx = edge_ref.shape
    by, bz = lines - 4, planes - 4
    part = by // ranks

    def middle_of(line):
        if 2 <= line < by + 2:
            k, j = divmod(line - 2, part)
            return own_ref[k, :, j * bx : (j + 1) * bx]
        index, j = (0, line) if line < 2 else (1, line - by - 2)
        return beside_ref[index, :, j * bx : (j + 1) * bx]

    me = lax.axis_index("gz")
    at_y = lax.axis_index("gy")
    at_x = lax.axis_index("gx")
    in_left = in_left_ref[...]
    out_left = out_left_ref[...]
    in_bias = in_bias_ref[:, 0:1]
    out_bias = out_bias_ref[:, 0:1]
    for y in range(by + 2):
        seg_taps[y, pl.ds(15, planes, stride=16), :] = jnp.zeros((planes, bx), F32)
    lane = lane_of((planes, bx))
    for line in range(lines):
        middle, edge = middle_of(line), edge_ref[line]
        for s in range(5):
            value = middle
            if s < 2:
                value = pltpu.roll(jnp.where(lane >= bx - (2 - s), edge, middle), 2 - s, 1)
            if s > 2:
                value = pltpu.roll(jnp.where(lane < s - 2, edge, middle), bx - (s - 2), 1)
            for b in range(3):
                if 0 <= line - b < by + 2:
                    seg_taps[line - b, pl.ds(b * 5 + s, planes, stride=16), :] = value

    for z in range(bz):
        for y in range(by):
            clean_ref[z, y : y + 1, :] = middle_of(2 + y)[2 + z : 3 + z]
    shape = (48, (by + 2) * bx)
    lane, row = lane_of(shape), row_of(shape)
    place_y = at_y * by + lane // bx - 1
    place_x = at_x * bx + lane % bx + row // 16 - 1
    inside = (place_y >= 0) & (place_y < gy * by) & (place_x >= 0) & (place_x < gx * bx)
    mask = jnp.where(inside, 1.0, 0.0).astype(F32)
    partial = []
    for z in range(bz + 2):
        rows = jnp.concatenate([seg_taps[y, z * 16 : z * 16 + 48, :] for y in range(by + 2)], axis=1)
        high, low = split(rows)
        grown = jnp.maximum(mxu(in_left, right_rows(high, low)) + in_bias, 0.0) * mask
        if z == 0:
            grown = grown * jnp.where(me > 0, 1.0, 0.0).astype(F32)
        if z == bz + 1:
            grown = grown * jnp.where(me < gz - 1, 1.0, 0.0).astype(F32)
        high, low = split(grown)
        field_high = jnp.concatenate([high[:, b * bx : (b + by) * bx] for b in range(3)], axis=0)
        field_low = jnp.concatenate([low[:, b * bx : (b + by) * bx] for b in range(3)], axis=0)
        partial.append(mxu(out_left, right_rows(field_high, field_low)))
        if z >= 2:
            total = partial[z - 2][0:16] + partial[z - 1][16:32] + partial[z][32:48] + out_bias
            for y in range(by):
                result[pl.ds((z - 2) * by + y, 16, stride=bz * by), :] = total[:, y * bx : (y + 1) * bx]
    out_ref[...] = result[0 : 16 * bz * by, :]


def body(sizes, noisy, first_weight, first_bias, second_weight, second_bias, head_weight,
         seg_weight_in, seg_bias_in, seg_weight_out, seg_bias_out):
    gz, gy, gx = sizes
    bz, by, bx = noisy.shape
    ranks = by // 4
    part = by // ranks
    lines = part + 4
    depth = gz * bz
    args = [
        noisy.reshape(bz * by, bx),
        first_weight.transpose(2, 1, 0),
        first_bias.reshape(1, -1),
        second_weight.transpose(2, 1, 0),
        second_bias.reshape(1, -1),
        head_weight.reshape(1, -1),
        seg_weight_in,
        seg_bias_in.reshape(1, -1),
        seg_weight_out,
        seg_bias_out.reshape(1, -1),
    ]
    vmem = pl.BlockSpec(memory_space=pltpu.VMEM)
    dma = pltpu.SemaphoreType.DMA
    rest = pl.BlockSpec(memory_space=pl.ANY)

    def room(*shape):
        return pltpu.VMEM(shape, F32)

    stages = [
        room(*(a.shape if i not in (1, 6) else (a.shape[0], a.shape[2]))) for i, a in enumerate(args)
    ]
    handed = pl.pallas_call(
        functools.partial(layers_kernel, sizes, ranks, bz, by, bx),
        out_shape=[
            room(ranks, bz + 4, part * bx),
            room(2, bz + 4, 2 * bx),
            room(by + 4, bz + 4, bx),
            pltpu.VMEM((48, 144), BF16),
            pltpu.VMEM((48, 432), BF16),
            room(48, LANES),
            room(16, LANES),
        ],
        in_specs=[rest] * len(args),
        out_specs=[vmem] * 7,
        scratch_shapes=stages
        + [
            dma((len(args),)),
            room(depth * by, bx),
            room(2, depth * 2, bx),
            room(3, 2, gz, by, bx),
            room(2, bz * 2, bx),
            room(by, bx),
            dma((6, max(ranks, 2))),
            dma((9, gz)),
            room(6, (depth + 2) * lines, bx),
            room(2, min(depth, 16), 16 * (part + 2), 2 * bx),
            room(depth + 2, 96, part * bx),
            room(depth + 16, part * bx),
            room(gz, bz + 4, part * bx),
            room(gz, bz + 4, bx),
            room(ranks + 2, 2, bz + 4, bx),
            dma((gz,)),
            dma((ranks,)),
            dma((2, gz)),
            dma((2,)),
            dma((2, gz)),
            dma((2, 2, gz)),
            dma((ranks + 2, 2)),
        ],
        compiler_params=pltpu.CompilerParams(
            collective_id=0, has_side_effects=True, vmem_limit_bytes=GRANT
        ),
        name="layers",
    )(*(pltpu.with_memory_space_constraint(a, pltpu.HBM) for a in args))
    clean, features = pl.pallas_call(
        functools.partial(segment_kernel, sizes),
        out_shape=[
            jax.ShapeDtypeStruct((bz, by, bx), F32),
            jax.ShapeDtypeStruct((16 * bz * by, bx), F32),
        ],
        in_specs=[vmem] * 7,
        out_specs=[vmem] * 2,
        scratch_shapes=[room(by + 2, (bz + 5) * 16, bx), room(17 * bz * by, bx)],
        compiler_params=pltpu.CompilerParams(vmem_limit_bytes=GRANT),
        name="segment",
    )(*handed)
    return clean, features.reshape(16, bz, by, bx)


def solution(mesh):
    sizes = (mesh.shape["gz"], mesh.shape["gy"], mesh.shape["gx"])
    in_specs = (P(("win", "gz"), "gy", "gx"), P(), P(), P(), P(), P(), P(), P(), P(), P())
    out_specs = (P(("win", "gz"), "gy", "gx"), P(None, ("win", "gz"), "gy", "gx"))
    return jax.shard_map(
        functools.partial(body, sizes), mesh=mesh, in_specs=in_specs, out_specs=out_specs, check_vma=False
    )
```

time: 22.1 us -> 18.6 us (0.84)
  Pallas kernels: 21.2 us -> 17.7 us
    pallas_call x1, Pallas kernels: 18.3 us -> 14.8 us  [body(): pl.pallas_call(functools.partial(layers_kernel, sizes, ranks, bz, by, bx)...]
where the time goes in v3:
time: 18.6 us; the launch traced here: 18.3 us
  Pallas kernels  17.7 us (95%)
  between operations  0.64 us (3%)
    pallas_call x1, Pallas kernels, body(): pl.pallas_call(functools.partial(layers_kernel, sizes, ranks, bz, by, bx)...  14.8 us
    pallas_call x1, Pallas kernels, body(): pl.pallas_call(functools.partial(segment_kernel, sizes), out_shape=[jax.S...  2.83 us

profile of v3, /device:TPU:0, one launch (start us, length us, event | category | flops | bytes accessed | tf_op | source)
XLA Modules:
  0.0 18.3 jit_solution(17489434266717208668)
XLA Ops:
  0.6 14.8 %layers.1 = (f32[2,8,512]{2,1,0:T(8,128)S(1)}, f32[2,8,256]{2,1,0:T(8,128)S(1)}, f32[12,8,128]{2,1,0:T(8,128)S(1)}, bf16[48,144]{1,0:T(8,128)(2,1)S(1)}, bf16[48...) custom-call(f32[32,128]{1,0:T(8,128)} %bitcast.10, f32[27,1,32]{2,1,0:T(1,128)} %bitcast.11, ...), custom_call_target="tpu_custom_call" | custom-call | tf_op jit(solution)/shard_map/layers/pallas_call | solution.py:671
  15.5 2.8 %segment.1 = (f32[4,8,128]{2,1,0:T(8,128)}, f32[512,128]{1,0:T(8,128)}) custom-call(f32[2,8,512]{2,1,0:T(8,128)S(1)} %get-tuple-element.11.own_ref, f32[2,8,256]{2,1,0:T(8,128)S(1)} %get-tuple-element.12.beside_ref, f32[12,8,128]{2,1,0:T(8,128)S(1)} %get-tuple-element.13.edge_ref, bf16[48,144]{1,0:T(8,128)(2,1)S(1)} %get-tuple-element.14.in_left_ref, ...), custom_call_target="tpu_custom_call" | custom-call | tf_op jit(solution)/shard_map/segment/pallas_call | solution.py:714

commit v4 on v3

--- a/solution.py
+++ b/solution.py
@@ -168,6 +168,8 @@
     at_y = lax.axis_index("gy")
     at_x = lax.axis_index("gx")
     works = me < ranks
+    turned_round = 1 - lax.rem(at_y, 2)
+    mine = me + turned_round * (ranks - 1 - 2 * me)
     steps_y = (-1, 1) if gy > 1 else ()
     steps_x = (-1, 1) if gx > 1 else ()
 
@@ -202,6 +204,10 @@
 
     def rank_towards(dy):
         return 0 if dy > 0 else ranks - 1
+
+    def home_towards(dy):
+        rank = rank_towards(dy)
+        return rank + (1 - turned_round) * (ranks - 1 - 2 * rank)
 
     def side(step):
         return (step + 1) // 2
@@ -231,11 +237,11 @@
             if (dy, dx, k) != (0, 0, 0):
                 pl.semaphore_signal(barrier, inc=1, device_id=device(peer(k), dy, dx), device_id_type=MESH)
 
+    for dy in steps_y:
+        for dx in (0,) + steps_x:
+            when(both(mine == rank_towards(-dy), exists(dy, dx)), functools.partial(greet, dy, dx))
     for dx in (0,) + steps_x:
         when(both(works, exists(0, dx)), functools.partial(greet, 0, dx))
-    for dy in steps_y:
-        for dx in (0,) + steps_x:
-            when(both(me == rank_towards(-dy), exists(dy, dx)), functools.partial(greet, dy, dx))
     for load in loads[1:]:
         load.start()
 
@@ -275,7 +281,7 @@
             dst_ref=my.at[side(-dy), rows_of(source, bz * 2), :],
             send_sem=send1.at[1, side(dy)],
             recv_sem=recv1.at[1 + side(-dy), source],
-            device_id=device(rank_towards(dy), dy, 0),
+            device_id=device(home_towards(dy), dy, 0),
             device_id_type=MESH,
         )
 
@@ -295,7 +301,7 @@
             dst_ref=x1.at[1 + side(-dy), side(-dx), source],
             send_sem=send1.at[4 + side(dy), side(dx)],
             recv_sem=recv1.at[5 + 2 * side(-dy) + side(-dx), source],
-            device_id=device(rank_towards(dy), dy, dx),
+            device_id=device(home_towards(dy), dy, dx),
             device_id_type=MESH,
         )
 
@@ -375,16 +381,19 @@
 
     late = []
     for target in range(gz):
-        late.append((me != target, functools.partial(own_last, me, target)))
+        late.append((me != target, functools.partial(own_last, mine, target)))
         for dy in steps_y:
-            ok = both(me == rank_towards(-dy), exists(dy, 0))
+            ok = both(mine == rank_towards(-dy), exists(dy, 0))
             late.append((ok, functools.partial(halo_last, dy, target)))
         for dx in steps_x:
-            late.append((exists(0, dx), functools.partial(edge_last, dx, me, target)))
+            late.append((exists(0, dx), functools.partial(edge_last, dx, mine, target)))
         for dy in steps_y:
             for dx in steps_x:
-                ok = both(me == rank_towards(-dy), exists(dy, dx))
+                ok = both(mine == rank_towards(-dy), exists(dy, dx))
                 late.append((ok, functools.partial(corner_last, dy, dx, target)))
+
+    for ok, make in early:
+        when(ok, lambda make=make: make(me).wait_send())
 
     @pl.when(works)
     def layers():
@@ -394,7 +403,7 @@
         head = column(head_ref)
         shape = (16 * rows, 2 * bx)
         lane, row = lane_of(shape), row_of(shape)
-        place_y = at_y * by + me * part + row // 16 - 1
+        place_y = at_y * by + mine * part + row // 16 - 1
         outside = (place_y < 0) | (place_y >= gy * by)
         outside = outside | ((at_x == 0) & (lane == 2 * bx - 1)) | ((at_x == gx - 1) & (lane == bx))
         mask = jnp.where(outside, 0.0, 1.0).astype(F32)
@@ -406,41 +415,40 @@
         fix[...] = jnp.zeros(fix.shape, F32)
         m1[rows_of(me, bz * by), :] = noisy_ref[...]
 
-        for k in range(1, gz):
-            own_first(0, peer(k)).wait_recv()
-        for dx in steps_x:
-            def await_edges(dx=dx):
-                for source in range(gz):
-                    edge_first(-dx, 0, source).wait_recv()
-            when(exists(0, dx), await_edges)
-        for dy in steps_y:
-            def await_halos(dy=dy):
-                for source in range(gz):
-                    halo_first(-dy, source).wait_recv()
-            when(both(me == rank_towards(-dy), exists(dy, 0)), await_halos)
+        def arrive(m):
+            def await_own():
+                own_first(0, m).wait_recv()
+            pl.when(me != m)(await_own)
             for dx in steps_x:
-                def await_corners(dy=dy, dx=dx):
-                    for source in range(gz):
-                        corner_first(-dy, -dx, source).wait_recv()
-                when(both(me == rank_towards(-dy), exists(dy, dx)), await_corners)
-
-        lane = lane_of((lines, bx))
+                def await_edge(dx=dx):
+                    edge_first(-dx, 0, m).wait_recv()
+                when(exists(0, dx), await_edge)
+            for dy in steps_y:
+                def await_halo(dy=dy):
+                    halo_first(-dy, m).wait_recv()
+                when(both(mine == rank_towards(-dy), exists(dy, 0)), await_halo)
+                for dx in steps_x:
+                    def await_corner(dy=dy, dx=dx):
+                        corner_first(-dy, -dx, m).wait_recv()
+                    when(both(mine == rank_towards(-dy), exists(dy, dx)), await_corner)
+
+        flat = lane_of((lines, bx))
         place = lane_of((by, bx)) % 4
 
-        def mine(full):
+        def cut(full):
             value = full[0:lines]
             for k in range(1, ranks):
-                value = jnp.where(me == k, full[part * k : part * k + lines], value)
+                value = jnp.where(mine == k, full[part * k : part * k + lines], value)
             return value
 
-        def gather(m, carry):
+        def gather(m):
             rims = [jnp.where(place < 2, x1[slot, 0, m], x1[slot, 1, m]) for slot in range(3)]
-            border = mine(jnp.concatenate([rims[1][by - 2 : by], rims[0], rims[2][0:2]], axis=0))
+            border = cut(jnp.concatenate([rims[1][by - 2 : by], rims[0], rims[2][0:2]], axis=0))
             below = my[0, rows_of(m, bz * 2), :]
             above = my[1, rows_of(m, bz * 2), :]
             block = m1[rows_of(m, bz * by), :]
             for z in range(bz):
-                value = mine(
+                value = cut(
                     jnp.concatenate(
                         [below[2 * z : 2 * z + 2], block[z * by : (z + 1) * by], above[2 * z : 2 * z + 2]],
                         axis=0,
@@ -448,15 +456,13 @@
                 )
                 beyond = pltpu.roll(border, (bx - 2 - 4 * z) % bx, 1)
                 where = pl.ds(aligned((m * bz + z + 1) * lines, lines), lines)
-                shifted[0, where, :] = pltpu.roll(jnp.where(lane == bx - 1, beyond, value), 1, 1)
+                shifted[0, where, :] = pltpu.roll(jnp.where(flat == bx - 1, beyond, value), 1, 1)
                 shifted[1, where, :] = value
-                shifted[2, where, :] = pltpu.roll(jnp.where(lane == 0, beyond, value), bx - 1, 1)
-                shifted[3, where, :] = pltpu.roll(jnp.where(lane == bx - 2, beyond, value), 1, 1)
+                shifted[2, where, :] = pltpu.roll(jnp.where(flat == 0, beyond, value), bx - 1, 1)
+                shifted[3, where, :] = pltpu.roll(jnp.where(flat == bx - 2, beyond, value), 1, 1)
                 shifted[4, where, :] = beyond
-                shifted[5, where, :] = pltpu.roll(jnp.where(lane == 1, beyond, value), bx - 1, 1)
-            return carry
-
-        times(gz, gather, 0)
+                shifted[5, where, :] = pltpu.roll(jnp.where(flat == 1, beyond, value), bx - 1, 1)
+
         lane = lane_of((16 * rows, bx))
         spare = jnp.ones((lines, bx), F32)
 
@@ -493,19 +499,21 @@
             product[z + 1] = mxu(second_left, right_rows(stacked(highs), stacked(lows)))
             return hidden
 
-        chunk = ready.shape[1]
-
-        def forward(step, hidden):
-            ahead = 16
-            for slot in range(min(ahead, chunk)):
-                gates(step * chunk + slot, slot)
-            for slot in range(chunk):
-                if slot + ahead < chunk:
-                    gates(step * chunk + slot + ahead, slot + ahead)
-                hidden = advance(step * chunk + slot, slot, hidden)
+        def reach(m, first, count, hidden):
+            arrive(m)
+            gather(m)
+            for slot in range(count):
+                gates(first + slot, slot)
+            for slot in range(count):
+                hidden = advance(first + slot, slot, hidden)
             return hidden
 
-        times(depth // chunk, forward, jnp.zeros((16 * rows, 2 * bx), F32))
+        def later(i, hidden):
+            return reach(i + 1, (i + 1) * bz - 1, bz, hidden)
+
+        hidden = reach(0, 0, bz - 1, jnp.zeros((16 * rows, 2 * bx), F32))
+        hidden = times(gz - 2, later, hidden)
+        reach(gz - 1, depth - bz - 1, bz + 1, hidden)
 
         def back(z, hidden):
             pre = product[z, 0:32] + product[z + 1, 32:64] + product[z + 2, 64:96]
@@ -529,15 +537,12 @@
             packed_rim[target] = border[bz * target : bz * target + bz + 4]
         for ok, make in late:
             when(ok, lambda make=make: make().start())
-        for k in range(ranks):
-            def keep(k=k):
-                own_ref[k] = packed[k]
-            pl.when(me == k)(keep)
+        own_ref[mine] = packed[me]
 
     for k in range(ranks):
         def await_own(k=k):
             own_last(k, 0).wait_recv()
-        pl.when(me != k)(await_own)
+        pl.when(mine != k)(await_own)
     for dy in steps_y:
         def await_beside(dy=dy):
             halo_last(-dy, 0).wait_recv()
@@ -561,8 +566,6 @@
             slot, j = ranks + 1, line - by - 2
         beyond = jnp.where(place < 2, x3[slot, 0], x3[slot, 1])
         edge_ref[line] = pltpu.roll(beyond, (bx - 2 - 4 * j) % bx, 1)
-    for ok, make in early:
-        when(ok, lambda make=make: make(me).wait_send())
 
     @pl.when(works)
     def drain():
@@ -692,7 +695,7 @@
             dma((6, max(ranks, 2))),
             dma((9, gz)),
             room(6, (depth + 2) * lines, bx),
-            room(2, min(depth, 16), 16 * (part + 2), 2 * bx),
+            room(2, bz + 1, 16 * (part + 2), 2 * bx),
             room(depth + 2, 96, part * bx),
             room(depth + 16, part * bx),
             room(gz, bz + 4, part * bx),

time: 18.6 us -> 17.7 us (0.952)
  Pallas kernels: 17.7 us -> 16.8 us
    pallas_call x1, Pallas kernels: 14.8 us -> 14 us  [body(): pl.pallas_call(functools.partial(layers_kernel, sizes, ranks, bz, by, bx)...]
where the time goes in v4:
time: 17.7 us; the launch traced here: 17.4 us
  Pallas kernels  16.8 us (95%)
  between operations  0.64 us (4%)
    pallas_call x1, Pallas kernels, body(): pl.pallas_call(functools.partial(layers_kernel, sizes, ranks, bz, by, bx)...  14 us
    pallas_call x1, Pallas kernels, body(): pl.pallas_call(functools.partial(segment_kernel, sizes), out_shape=[jax.S...  2.83 us

profile of v4, /device:TPU:0, one launch (start us, length us, event | category | flops | bytes accessed | tf_op | source)
XLA Modules:
  0.0 17.4 jit_solution(1617546242756630797)
XLA Ops:
  0.6 14.0 %layers.1 = (f32[2,8,512]{2,1,0:T(8,128)S(1)}, f32[2,8,256]{2,1,0:T(8,128)S(1)}, f32[12,8,128]{2,1,0:T(8,128)S(1)}, bf16[48,144]{1,0:T(8,128)(2,1)S(1)}, bf16[48...) custom-call(f32[32,128]{1,0:T(8,128)} %bitcast.10, f32[27,1,32]{2,1,0:T(1,128)} %bitcast.11, ...), custom_call_target="tpu_custom_call" | custom-call | tf_op jit(solution)/shard_map/layers/pallas_call | solution.py:674
  14.6 2.8 %segment.1 = (f32[4,8,128]{2,1,0:T(8,128)}, f32[512,128]{1,0:T(8,128)}) custom-call(f32[2,8,512]{2,1,0:T(8,128)S(1)} %get-tuple-element.11.own_ref, f32[2,8,256]{2,1,0:T(8,128)S(1)} %get-tuple-element.12.beside_ref, f32[12,8,128]{2,1,0:T(8,128)S(1)} %get-tuple-element.13.edge_ref, bf16[48,144]{1,0:T(8,128)(2,1)S(1)} %get-tuple-element.14.in_left_ref, ...), custom_call_target="tpu_custom_call" | custom-call | tf_op jit(solution)/shard_map/segment/pallas_call | solution.py:717

commit v5 on v4

--- a/solution.py
+++ b/solution.py
@@ -63,53 +63,35 @@
     return jnp.where(left == right, 1.0, 0.0).astype(BF16)
 
 
-def spread_narrow(weight, shift):
-    taps = weight.shape[1]
-    shape = (taps, 48)
-    tap, col = row_of(shape), lane_of(shape)
+def tap_parts(tap):
     plane = (tap >= 9).astype(jnp.int32) + (tap >= 18).astype(jnp.int32)
     rest = tap - 9 * plane
     line = (rest >= 3).astype(jnp.int32) + (rest >= 6).astype(jnp.int32)
-    place = matches(col, tap + 7 * plane + 2 * line + shift)
-    return tuple(mxu(part, place).astype(BF16) for part in split(weight))
-
-
-def narrow_left(weight):
-    parts = weight.shape[0] // 16
-    highs, lows = [], []
-    for part in range(parts):
-        for shift in range(3):
-            high, low = spread_narrow(weight[16 * part : 16 * part + 16], shift)
-            highs.append(high)
-            lows.append(low)
-    high, low = jnp.concatenate(highs, axis=0), jnp.concatenate(lows, axis=0)
-    return jnp.concatenate([high, high, low], axis=1)
-
-
-def first_rows(weight, bias, lines):
-    taps = weight.shape[1]
-    block = 10 * (lines + 4)
+    return plane, line, rest - 3 * line
+
+
+def banded_rows(weight, bias, count, over_planes):
+    outs, taps = weight.shape
+    size = count + 2
+    block = 10 * size
     shape = (taps, 3 * block)
-    tap, col = row_of(shape), lane_of(shape)
-    plane = (tap >= 9).astype(jnp.int32) + (tap >= 18).astype(jnp.int32)
-    rest = tap - 9 * plane
-    line = (rest >= 3).astype(jnp.int32) + (rest >= 6).astype(jnp.int32)
-    start = (lines + 4) * (3 * (rest - 3 * line) + plane) + line
+    plane, line, step = tap_parts(row_of(shape))
+    slow, fast = (line, plane) if over_planes else (plane, line)
+    start = size * (3 * step + slow) + fast
+    col = lane_of(shape)
     high, low = split(weight)
-    half = weight.shape[0] // 2
-    shape = (half, 3 * block)
+    shape = (outs, 3 * block)
     steady = jnp.zeros(shape, F32)
     for piece in range(3):
         piece_of = bias.astype(BF16).astype(F32)
-        steady = jnp.where(lane_of(shape) == 9 * (lines + 4) + piece, piece_of, steady)
+        steady = jnp.where(lane_of(shape) == 9 * size + piece, piece_of, steady)
         bias = bias - piece_of
-    steady = jnp.concatenate([jnp.zeros(shape, F32), steady], axis=0)
     parts = []
-    for at in range(lines + 2):
+    for at in range(count):
         first = matches(col, start + at) + matches(col, start + at + block)
         last = matches(col, start + at + 2 * block)
         parts.append((mxu(high, first) + mxu(low, last) + steady).astype(BF16))
-    return jnp.concatenate([p[:half] for p in parts] + [p[half:] for p in parts], axis=0)
+    return parts
 
 
 def second_rows(turned, ins):
@@ -131,29 +113,69 @@
     )
 
 
-def last_left(weight):
+def last_rows(weight):
     outs, ins, taps = weight.shape
     shape = (taps, taps * ins)
-    place = matches(row_of(shape), lane_of(shape) // ins)
+    plane, line, step = tap_parts(row_of(shape))
+    place = matches(3 * (3 * line + step) + plane, lane_of(shape) // ins)
     shape = (outs * ins, taps * ins)
     keep = (row_of(shape) % ins) == (lane_of(shape) % ins)
     shape = (outs, outs * ins)
-    gather = matches(row_of(shape), lane_of(shape) // ins)
+    collect = matches(row_of(shape), lane_of(shape) // ins)
     parts = []
     for part in split(weight.reshape(outs * ins, taps)):
         grown = jnp.where(keep, mxu(part, place), 0.0).astype(BF16)
-        parts.append(mxu(gather, grown).astype(BF16))
+        parts.append(mxu(collect, grown).astype(BF16))
     third = taps * ins // 3
     high, low = (
-        jnp.concatenate([p[:, third * a : third * (a + 1)] for a in range(3)], axis=0) for p in parts
+        jnp.concatenate([p[:, third * b : third * (b + 1)] for b in range(3)], axis=0) for p in parts
     )
     return jnp.concatenate([high, high, low], axis=1)
+
+
+def window_of(shifted, start, count, spare):
+    halves = [
+        jnp.concatenate([shifted[s, pl.ds(start, count), :] for s in three] + [spare], axis=0)
+        for three in (range(3), range(3, 6))
+    ]
+    return right_rows(*split(jnp.concatenate(halves, axis=1)))
+
+
+def store_shifts(shifted, where, value, beyond):
+    size = value.shape[1]
+    lane = lane_of(value.shape)
+    shifted[0, where, :] = pltpu.roll(jnp.where(lane == size - 1, beyond, value), 1, 1)
+    shifted[1, where, :] = value
+    shifted[2, where, :] = pltpu.roll(jnp.where(lane == 0, beyond, value), size - 1, 1)
+    shifted[3, where, :] = pltpu.roll(jnp.where(lane == size - 2, beyond, value), 1, 1)
+    shifted[4, where, :] = beyond
+    shifted[5, where, :] = pltpu.roll(jnp.where(lane == 1, beyond, value), size - 1, 1)
+
+
+def stacked_shifts(field, count):
+    size = field.shape[1] // 2
+    inner, outer = field[:, 0:size], field[:, size:]
+    lane = lane_of(inner.shape)
+    fields = (
+        pltpu.roll(jnp.where(lane == size - 1, outer, inner), 1, 1),
+        inner,
+        pltpu.roll(jnp.where(lane == 0, outer, inner), size - 1, 1),
+    )
+    return right_rows(
+        *(
+            jnp.concatenate(
+                [jnp.concatenate([v[16 * j : 16 * j + 48] for j in range(count)], axis=1) for v in values],
+                axis=0,
+            )
+            for values in zip(*(split(f) for f in fields))
+        )
+    )
 
 
 def layers_kernel(
     sizes, ranks, bz, by, bx,
     noisy_any, w1_any, b1_any, w2_any, b2_any, head_any, w3_any, b3_any, w4_any, b4_any,
-    own_ref, beside_ref, edge_ref, in_left_ref, out_left_ref, in_bias_ref, out_bias_ref,
+    own_ref, beside_ref, edge_ref, in_left_ref, out_left_ref, out_bias_ref,
     noisy_ref, w1_ref, b1_ref, w2_ref, b2_ref, head_ref, w3_ref, b3_ref, w4_ref, b4_ref, load_sem,
     m1, my, x1, halo, rim, send1, recv1,
     shifted, ready, product, fix, packed, packed_rim,
@@ -333,9 +355,10 @@
             for slot in range(ranks + 2):
                 x3[slot, index] = jnp.zeros(x3.shape[2:], F32)
         pl.when(ok)(no_side)
-    in_left_ref[...] = narrow_left(w3_ref[...])
-    out_left_ref[...] = last_left(w4_ref[...])
-    in_bias_ref[...] = jnp.broadcast_to(jnp.concatenate([column(b3_ref)] * 3, axis=0), in_bias_ref.shape)
+    in_left_ref[...] = jnp.concatenate(
+        banded_rows(w3_ref[...], column(b3_ref), bz + 2, True), axis=0
+    )
+    out_left_ref[...] = last_rows(w4_ref[...])
     out_bias_ref[...] = jnp.broadcast_to(column(b4_ref), out_bias_ref.shape)
 
     def own_last(k, target):
@@ -397,7 +420,9 @@
 
     @pl.when(works)
     def layers():
-        first_left = first_rows(w1_ref[...].T, column(b1_ref), part)
+        gate_bias = jnp.concatenate([jnp.zeros((16, 1), F32), column(b1_ref)], axis=0)
+        parts = banded_rows(w1_ref[...].T, gate_bias, rows, False)
+        first_left = jnp.concatenate([p[:16] for p in parts] + [p[16:] for p in parts], axis=0)
         second_left = second_rows(w2_ref[...].reshape(-1, w2_ref.shape[2]), w2_ref.shape[1])
         second_bias = column(b2_ref)
         head = column(head_ref)
@@ -432,7 +457,6 @@
                         corner_first(-dy, -dx, m).wait_recv()
                     when(both(mine == rank_towards(-dy), exists(dy, dx)), await_corner)
 
-        flat = lane_of((lines, bx))
         place = lane_of((by, bx)) % 4
 
         def cut(full):
@@ -456,47 +480,18 @@
                 )
                 beyond = pltpu.roll(border, (bx - 2 - 4 * z) % bx, 1)
                 where = pl.ds(aligned((m * bz + z + 1) * lines, lines), lines)
-                shifted[0, where, :] = pltpu.roll(jnp.where(flat == bx - 1, beyond, value), 1, 1)
-                shifted[1, where, :] = value
-                shifted[2, where, :] = pltpu.roll(jnp.where(flat == 0, beyond, value), bx - 1, 1)
-                shifted[3, where, :] = pltpu.roll(jnp.where(flat == bx - 2, beyond, value), 1, 1)
-                shifted[4, where, :] = beyond
-                shifted[5, where, :] = pltpu.roll(jnp.where(flat == 1, beyond, value), bx - 1, 1)
-
-        lane = lane_of((16 * rows, bx))
+                store_shifts(shifted, where, value, beyond)
+
         spare = jnp.ones((lines, bx), F32)
 
         def gates(z, slot):
-            window = pl.ds(aligned(z * lines, lines), 3 * lines)
-            halves = [
-                jnp.concatenate([shifted[s, window, :] for s in three] + [spare], axis=0)
-                for three in (range(3), range(3, 6))
-            ]
-            high, low = split(jnp.concatenate(halves, axis=1))
-            pre = mxu(first_left, right_rows(high, low))
+            pre = mxu(first_left, window_of(shifted, aligned(z * lines, lines), 3 * lines, spare))
             ready[0, slot] = mask * jnp.tanh(pre[0 : 16 * rows])
             ready[1, slot] = jax.nn.sigmoid(pre[16 * rows :])
 
         def advance(z, slot, hidden):
             hidden = hidden + ready[1, slot] * (ready[0, slot] - hidden)
-            inner, outer = hidden[:, 0:bx], hidden[:, bx:]
-            fields = (
-                pltpu.roll(jnp.where(lane == bx - 1, outer, inner), 1, 1),
-                inner,
-                pltpu.roll(jnp.where(lane == 0, outer, inner), bx - 1, 1),
-            )
-            highs, lows = zip(*(split(f) for f in fields))
-
-            def stacked(values):
-                return jnp.concatenate(
-                    [
-                        jnp.concatenate([v[16 * j : 16 * j + 48] for j in range(part)], axis=1)
-                        for v in values
-                    ],
-                    axis=0,
-                )
-
-            product[z + 1] = mxu(second_left, right_rows(stacked(highs), stacked(lows)))
+            product[z + 1] = mxu(second_left, stacked_shifts(hidden, part))
             return hidden
 
         def reach(m, first, count, hidden):
@@ -574,14 +569,17 @@
 
 
 def segment_kernel(
-    sizes, own_ref, beside_ref, edge_ref, in_left_ref, out_left_ref, in_bias_ref, out_bias_ref,
-    clean_ref, out_ref, seg_taps, result,
+    sizes, own_ref, beside_ref, edge_ref, in_left_ref, out_left_ref, out_bias_ref,
+    clean_ref, out_ref, shifted, ready, product, result,
 ):
     gz, gy, gx = sizes
     ranks = own_ref.shape[0]
     lines, planes, bx = edge_ref.shape
     by, bz = lines - 4, planes - 4
     part = by // ranks
+    me = lax.axis_index("gz")
+    at_y = lax.axis_index("gy")
+    at_x = lax.axis_index("gx")
 
     def middle_of(line):
         if 2 <= line < by + 2:
@@ -590,54 +588,33 @@
         index, j = (0, line) if line < 2 else (1, line - by - 2)
         return beside_ref[index, :, j * bx : (j + 1) * bx]
 
-    me = lax.axis_index("gz")
-    at_y = lax.axis_index("gy")
-    at_x = lax.axis_index("gx")
+    for line in range(lines):
+        store_shifts(shifted, slice(line * planes, (line + 1) * planes), middle_of(line), edge_ref[line])
     in_left = in_left_ref[...]
     out_left = out_left_ref[...]
-    in_bias = in_bias_ref[:, 0:1]
     out_bias = out_bias_ref[:, 0:1]
+    shape = (16 * (bz + 2), 2 * bx)
+    lane, plane = lane_of(shape), row_of(shape) // 16
+    outside = ((me == 0) & (plane == 0)) | ((me == gz - 1) & (plane == bz + 1))
+    outside = outside | ((at_x == 0) & (lane == 2 * bx - 1)) | ((at_x == gx - 1) & (lane == bx))
+    mask = jnp.where(outside, 0.0, 1.0).astype(F32)
+    spare = jnp.ones((planes, bx), F32)
     for y in range(by + 2):
-        seg_taps[y, pl.ds(15, planes, stride=16), :] = jnp.zeros((planes, bx), F32)
-    lane = lane_of((planes, bx))
-    for line in range(lines):
-        middle, edge = middle_of(line), edge_ref[line]
-        for s in range(5):
-            value = middle
-            if s < 2:
-                value = pltpu.roll(jnp.where(lane >= bx - (2 - s), edge, middle), 2 - s, 1)
-            if s > 2:
-                value = pltpu.roll(jnp.where(lane < s - 2, edge, middle), bx - (s - 2), 1)
-            for b in range(3):
-                if 0 <= line - b < by + 2:
-                    seg_taps[line - b, pl.ds(b * 5 + s, planes, stride=16), :] = value
-
+        grown = jnp.maximum(mxu(in_left, window_of(shifted, y * planes, 3 * planes, spare)), 0.0) * mask
+        if y == 0:
+            grown = grown * jnp.where(at_y > 0, 1.0, 0.0).astype(F32)
+        if y == by + 1:
+            grown = grown * jnp.where(at_y < gy - 1, 1.0, 0.0).astype(F32)
+        ready[y] = grown
     for z in range(bz):
         for y in range(by):
             clean_ref[z, y : y + 1, :] = middle_of(2 + y)[2 + z : 3 + z]
-    shape = (48, (by + 2) * bx)
-    lane, row = lane_of(shape), row_of(shape)
-    place_y = at_y * by + lane // bx - 1
-    place_x = at_x * bx + lane % bx + row // 16 - 1
-    inside = (place_y >= 0) & (place_y < gy * by) & (place_x >= 0) & (place_x < gx * bx)
-    mask = jnp.where(inside, 1.0, 0.0).astype(F32)
-    partial = []
-    for z in range(bz + 2):
-        rows = jnp.concatenate([seg_taps[y, z * 16 : z * 16 + 48, :] for y in range(by + 2)], axis=1)
-        high, low = split(rows)
-        grown = jnp.maximum(mxu(in_left, right_rows(high, low)) + in_bias, 0.0) * mask
-        if z == 0:
-            grown = grown * jnp.where(me > 0, 1.0, 0.0).astype(F32)
-        if z == bz + 1:
-            grown = grown * jnp.where(me < gz - 1, 1.0, 0.0).astype(F32)
-        high, low = split(grown)
-        field_high = jnp.concatenate([high[:, b * bx : (b + by) * bx] for b in range(3)], axis=0)
-        field_low = jnp.concatenate([low[:, b * bx : (b + by) * bx] for b in range(3)], axis=0)
-        partial.append(mxu(out_left, right_rows(field_high, field_low)))
-        if z >= 2:
-            total = partial[z - 2][0:16] + partial[z - 1][16:32] + partial[z][32:48] + out_bias
-            for y in range(by):
-                result[pl.ds((z - 2) * by + y, 16, stride=bz * by), :] = total[:, y * bx : (y + 1) * bx]
+    for y in range(by + 2):
+        product[y] = mxu(out_left, stacked_shifts(ready[y], bz))
+        if y >= 2:
+            total = product[y - 2, 0:16] + product[y - 1, 16:32] + product[y, 32:48] + out_bias
+            for z in range(bz):
+                result[pl.ds(z * by + y - 2, 16, stride=bz * by), :] = total[:, z * bx : (z + 1) * bx]
     out_ref[...] = result[0 : 16 * bz * by, :]
 
 
@@ -677,13 +654,12 @@
             room(ranks, bz + 4, part * bx),
             room(2, bz + 4, 2 * bx),
             room(by + 4, bz + 4, bx),
-            pltpu.VMEM((48, 144), BF16),
+            pltpu.VMEM((16 * (bz + 2), 30 * (bz + 4)), BF16),
             pltpu.VMEM((48, 432), BF16),
-            room(48, LANES),
             room(16, LANES),
         ],
         in_specs=[rest] * len(args),
-        out_specs=[vmem] * 7,
+        out_specs=[vmem] * 6,
         scratch_shapes=stages
         + [
             dma((len(args),)),
@@ -720,9 +696,14 @@
             jax.ShapeDtypeStruct((bz, by, bx), F32),
             jax.ShapeDtypeStruct((16 * bz * by, bx), F32),
         ],
-        in_specs=[vmem] * 7,
+        in_specs=[vmem] * 6,
         out_specs=[vmem] * 2,
-        scratch_shapes=[room(by + 2, (bz + 5) * 16, bx), room(17 * bz * by, bx)],
+        scratch_shapes=[
+            room(6, (by + 4) * (bz + 4), bx),
+            room(by + 2, 16 * (bz + 2), 2 * bx),
+            room(by + 2, 48, bz * bx),
+            room(17 * bz * by, bx),
+        ],
         compiler_params=pltpu.CompilerParams(vmem_limit_bytes=GRANT),
         name="segment",
     )(*handed)

time: 17.7 us -> 16.9 us (0.955)
  Pallas kernels: 16.8 us -> 16 us
    pallas_call x1, Pallas kernels: 2.83 us -> 2.03 us  [body(): pl.pallas_call(functools.partial(segment_kernel, sizes), out_shape=[jax.S...]
where the time goes in v5:
time: 16.9 us; the launch traced here: 16.6 us
  Pallas kernels  16 us (95%)
  between operations  0.64 us (4%)
    pallas_call x1, Pallas kernels, body(): pl.pallas_call(functools.partial(layers_kernel, sizes, ranks, bz, by, bx)...  14 us
    pallas_call x1, Pallas kernels, body(): pl.pallas_call(functools.partial(segment_kernel, sizes), out_shape=[jax.S...  2.03 us

profile of v5, /device:TPU:0, one launch (start us, length us, event | category | flops | bytes accessed | tf_op | source)
XLA Modules:
  0.0 16.6 jit_solution(3166712622440732816)
XLA Ops:
  0.6 14.0 %layers.1 = (f32[2,8,512]{2,1,0:T(8,128)S(1)}, f32[2,8,256]{2,1,0:T(8,128)S(1)}, f32[12,8,128]{2,1,0:T(8,128)S(1)}, bf16[96,240]{1,0:T(8,128)(2,1)S(1)}, bf16[48...) custom-call(f32[32,128]{1,0:T(8,128)} %bitcast.10, f32[27,1,32]{2,1,0:T(1,128)} %bitcast.11, f32[1,16]{1,0:T(1,128)} %bitcast.12, ...), custom_call_target="tpu_custom_call" | custom-call | tf_op jit(solution)/shard_map/layers/pallas_call | solution.py:651
  14.6 2.0 %segment.1 = (f32[4,8,128]{2,1,0:T(8,128)}, f32[512,128]{1,0:T(8,128)}) custom-call(f32[2,8,512]{2,1,0:T(8,128)S(1)} %get-tuple-element.10.own_ref, f32[2,8,256]{2,1,0:T(8,128)S(1)} %get-tuple-element.11.beside_ref, f32[12,8,128]{2,1,0:T(8,128)S(1)} %get-tuple-element.12.edge_ref, bf16[96,240]{1,0:T(8,128)(2,1)S(1)} %get-tuple-element.13.in_left_ref, ...), custom_call_target="tpu_custom_call" | custom-call | tf_op jit(solution)/shard_map/segment/pallas_call | solution.py:693

commit v6 on v5

--- a/solution.py
+++ b/solution.py
@@ -53,6 +53,25 @@
             carry = step(count - 1 - i if backward else i, carry)
         return carry
     return lax.fori_loop(0, count, lambda i, c: step(count - 1 - i if backward else i, c), carry)
+
+
+class Step:
+    def __init__(self, step, side, ok):
+        self.step, self.side, self.ok = step, side, ok
+
+    def back(self):
+        return Step(-self.step, 1 - self.side, self.ok)
+
+
+def steps_along(at, count):
+    if count == 1:
+        return []
+    if count == 2:
+        return [Step(1 - 2 * at, 1 - at, None)]
+    return [Step(-1, 0, at > 0), Step(1, 1, at < count - 1)]
+
+
+STAY = Step(0, 0, None)
 
 
 def aligned(start, unit):
@@ -130,7 +149,7 @@
     high, low = (
         jnp.concatenate([p[:, third * b : third * (b + 1)] for b in range(3)], axis=0) for p in parts
     )
-    return jnp.concatenate([high, high, low], axis=1)
+    return jnp.concatenate([high, low], axis=0)
 
 
 def window_of(shifted, start, count, spare):
@@ -161,14 +180,12 @@
         inner,
         pltpu.roll(jnp.where(lane == 0, outer, inner), size - 1, 1),
     )
-    return right_rows(
-        *(
-            jnp.concatenate(
-                [jnp.concatenate([v[16 * j : 16 * j + 48] for j in range(count)], axis=1) for v in values],
-                axis=0,
-            )
-            for values in zip(*(split(f) for f in fields))
-        )
+    return tuple(
+        jnp.concatenate(
+            [jnp.concatenate([v[16 * j : 16 * j + 48] for j in range(count)], axis=1) for v in values],
+            axis=0,
+        )
+        for values in zip(*(split(f) for f in fields))
     )
 
 
@@ -192,17 +209,8 @@
     works = me < ranks
     turned_round = 1 - lax.rem(at_y, 2)
     mine = me + turned_round * (ranks - 1 - 2 * me)
-    steps_y = (-1, 1) if gy > 1 else ()
-    steps_x = (-1, 1) if gx > 1 else ()
-
-    def exists(dy, dx):
-        ok = None
-        for where, step, count in ((at_y, dy, gy), (at_x, dx, gx)):
-            if step == 0:
-                continue
-            here = where > 0 if step < 0 else where < count - 1
-            ok = here if ok is None else ok & here
-        return ok
+    steps_y = steps_along(at_y, gy)
+    steps_x = steps_along(at_x, gx)
 
     def both(first, second):
         return second if first is None else first if second is None else first & second
@@ -217,22 +225,22 @@
         return {
             "win": lax.axis_index("win"),
             "gz": z,
-            "gy": lax.rem(at_y + dy + gy, gy),
-            "gx": lax.rem(at_x + dx + gx, gx),
+            "gy": lax.rem(at_y + dy.step + gy, gy),
+            "gx": lax.rem(at_x + dx.step + gx, gx),
         }
 
     def peer(k):
         return lax.rem(me + k, gz)
 
     def rank_towards(dy):
-        return 0 if dy > 0 else ranks - 1
+        return (1 - dy.side) * (ranks - 1)
+
+    def beside(dy):
+        return both(mine == rank_towards(dy.back()), dy.ok)
 
     def home_towards(dy):
         rank = rank_towards(dy)
         return rank + (1 - turned_round) * (ranks - 1 - 2 * rank)
-
-    def side(step):
-        return (step + 1) // 2
 
     loads = [
         pltpu.make_async_copy(source, target, load_sem.at[i])
@@ -255,15 +263,20 @@
     barrier = pltpu.get_barrier_semaphore()
 
     def greet(dy, dx):
-        for k in range(gz - 1, -1, -1):
-            if (dy, dx, k) != (0, 0, 0):
-                pl.semaphore_signal(barrier, inc=1, device_id=device(peer(k), dy, dx), device_id_type=MESH)
+        for k in range(gz - 1, 0 if dy is STAY and dx is STAY else -1, -1):
+            pl.semaphore_signal(barrier, inc=1, device_id=device(peer(k), dy, dx), device_id_type=MESH)
 
     for dy in steps_y:
-        for dx in (0,) + steps_x:
-            when(both(mine == rank_towards(-dy), exists(dy, dx)), functools.partial(greet, dy, dx))
-    for dx in (0,) + steps_x:
-        when(both(works, exists(0, dx)), functools.partial(greet, 0, dx))
+        @functools.partial(when, beside(dy))
+        def greet_beside(dy=dy):
+            for dx in [STAY] + steps_x:
+                when(dx.ok, functools.partial(greet, dy, dx))
+
+    @pl.when(works)
+    def greet_along():
+        for dx in [STAY] + steps_x:
+            when(dx.ok, functools.partial(greet, STAY, dx))
+
     for load in loads[1:]:
         load.start()
 
@@ -293,49 +306,49 @@
             dst_ref=m1.at[rows_of(source, bz * by), :],
             send_sem=send1.at[0, k],
             recv_sem=recv1.at[0, source],
-            device_id=device(k, 0, 0),
+            device_id=device(k, STAY, STAY),
             device_id_type=MESH,
         )
 
     def halo_first(dy, source):
         return pltpu.make_async_remote_copy(
-            src_ref=halo.at[side(dy)],
-            dst_ref=my.at[side(-dy), rows_of(source, bz * 2), :],
-            send_sem=send1.at[1, side(dy)],
-            recv_sem=recv1.at[1 + side(-dy), source],
-            device_id=device(home_towards(dy), dy, 0),
+            src_ref=halo.at[dy.side],
+            dst_ref=my.at[1 - dy.side, rows_of(source, bz * 2), :],
+            send_sem=send1.at[1, dy.side],
+            recv_sem=recv1.at[2 - dy.side, source],
+            device_id=device(home_towards(dy), dy, STAY),
             device_id_type=MESH,
         )
 
     def edge_first(dx, k, source):
         return pltpu.make_async_remote_copy(
             src_ref=rim,
-            dst_ref=x1.at[0, side(-dx), source],
-            send_sem=send1.at[2 + side(dx), k],
-            recv_sem=recv1.at[3 + side(-dx), source],
-            device_id=device(k, 0, dx),
+            dst_ref=x1.at[0, 1 - dx.side, source],
+            send_sem=send1.at[2 + dx.side, k],
+            recv_sem=recv1.at[4 - dx.side, source],
+            device_id=device(k, STAY, dx),
             device_id_type=MESH,
         )
 
     def corner_first(dy, dx, source):
         return pltpu.make_async_remote_copy(
             src_ref=rim,
-            dst_ref=x1.at[1 + side(-dy), side(-dx), source],
-            send_sem=send1.at[4 + side(dy), side(dx)],
-            recv_sem=recv1.at[5 + 2 * side(-dy) + side(-dx), source],
+            dst_ref=x1.at[2 - dy.side, 1 - dx.side, source],
+            send_sem=send1.at[4 + dy.side, dx.side],
+            recv_sem=recv1.at[8 - 2 * dy.side - dx.side, source],
             device_id=device(home_towards(dy), dy, dx),
             device_id_type=MESH,
         )
 
     early = []
     for dy in steps_y:
-        early.append((exists(dy, 0), functools.partial(halo_first, dy)))
+        early.append((dy.ok, functools.partial(halo_first, dy)))
         for dx in steps_x:
-            early.append((exists(dy, dx), functools.partial(corner_first, dy, dx)))
+            early.append((both(dy.ok, dx.ok), functools.partial(corner_first, dy, dx)))
     for k in range(ranks):
         early.append((me != k, functools.partial(own_first, k)))
         for dx in steps_x:
-            early.append((exists(0, dx), functools.partial(edge_first, dx, k)))
+            early.append((dx.ok, functools.partial(edge_first, dx, k)))
     for ok, make in early:
         when(ok, lambda make=make: make(me).start())
 
@@ -367,53 +380,66 @@
             dst_ref=own_ref.at[k],
             send_sem=own_send.at[target],
             recv_sem=own_recv.at[k],
-            device_id=device(target, 0, 0),
+            device_id=device(target, STAY, STAY),
             device_id_type=MESH,
         )
 
     def halo_last(dy, target):
-        start = 0 if dy < 0 else (part - 2) * bx
+        start = aligned(dy.side * ((part - 2) * bx), LANES)
         return pltpu.make_async_remote_copy(
-            src_ref=packed.at[target, :, start : start + 2 * bx],
-            dst_ref=beside_ref.at[side(-dy)],
-            send_sem=beside_send.at[side(dy), target],
-            recv_sem=beside_recv.at[side(-dy)],
-            device_id=device(target, dy, 0),
+            src_ref=packed.at[target, :, pl.ds(start, 2 * bx)],
+            dst_ref=beside_ref.at[1 - dy.side],
+            send_sem=beside_send.at[dy.side, target],
+            recv_sem=beside_recv.at[1 - dy.side],
+            device_id=device(target, dy, STAY),
             device_id_type=MESH,
         )
 
     def edge_last(dx, k, target):
         return pltpu.make_async_remote_copy(
             src_ref=packed_rim.at[target],
-            dst_ref=x3.at[k, side(-dx)],
-            send_sem=edge_send.at[side(dx), target],
-            recv_sem=edge_recv.at[k, side(-dx)],
-            device_id=device(target, 0, dx),
+            dst_ref=x3.at[k, 1 - dx.side],
+            send_sem=edge_send.at[dx.side, target],
+            recv_sem=edge_recv.at[k, 1 - dx.side],
+            device_id=device(target, STAY, dx),
             device_id_type=MESH,
         )
 
     def corner_last(dy, dx, target):
         return pltpu.make_async_remote_copy(
             src_ref=packed_rim.at[target],
-            dst_ref=x3.at[ranks + side(-dy), side(-dx)],
-            send_sem=corner_send.at[side(dy), side(dx), target],
-            recv_sem=edge_recv.at[ranks + side(-dy), side(-dx)],
+            dst_ref=x3.at[ranks + 1 - dy.side, 1 - dx.side],
+            send_sem=corner_send.at[dy.side, dx.side, target],
+            recv_sem=edge_recv.at[ranks + 1 - dy.side, 1 - dx.side],
             device_id=device(target, dy, dx),
             device_id_type=MESH,
         )
 
-    late = []
-    for target in range(gz):
-        late.append((me != target, functools.partial(own_last, mine, target)))
+    def late(act):
+        def to_beside(dy, targets):
+            for target in targets:
+                act(halo_last(dy, target))
+                for dx in steps_x:
+                    when(dx.ok, lambda: act(corner_last(dy, dx, target)))
+
+        def to_own(target):
+            act(own_last(mine, target))
+
+        def to_edge(target):
+            for dx in steps_x:
+                when(dx.ok, lambda: act(edge_last(dx, mine, target)))
+
         for dy in steps_y:
-            ok = both(mine == rank_towards(-dy), exists(dy, 0))
-            late.append((ok, functools.partial(halo_last, dy, target)))
-        for dx in steps_x:
-            late.append((exists(0, dx), functools.partial(edge_last, dx, mine, target)))
+            when(beside(dy), functools.partial(to_beside, dy, range(ranks)))
+        for k in range(1, ranks):
+            to_own(lax.rem(me + k, ranks))
+        for target in range(ranks):
+            to_edge(target)
+        for target in range(ranks, gz):
+            to_own(target)
+            to_edge(target)
         for dy in steps_y:
-            for dx in steps_x:
-                ok = both(mine == rank_towards(-dy), exists(dy, dx))
-                late.append((ok, functools.partial(corner_last, dy, dx, target)))
+            when(beside(dy), functools.partial(to_beside, dy, range(ranks, gz)))
 
     for ok, make in early:
         when(ok, lambda make=make: make(me).wait_send())
@@ -446,16 +472,16 @@
             pl.when(me != m)(await_own)
             for dx in steps_x:
                 def await_edge(dx=dx):
-                    edge_first(-dx, 0, m).wait_recv()
-                when(exists(0, dx), await_edge)
+                    edge_first(dx.back(), 0, m).wait_recv()
+                when(dx.ok, await_edge)
             for dy in steps_y:
-                def await_halo(dy=dy):
-                    halo_first(-dy, m).wait_recv()
-                when(both(mine == rank_towards(-dy), exists(dy, 0)), await_halo)
-                for dx in steps_x:
-                    def await_corner(dy=dy, dx=dx):
-                        corner_first(-dy, -dx, m).wait_recv()
-                    when(both(mine == rank_towards(-dy), exists(dy, dx)), await_corner)
+                @functools.partial(when, beside(dy))
+                def await_beside(dy=dy):
+                    halo_first(dy.back(), m).wait_recv()
+                    for dx in steps_x:
+                        def await_corner(dx=dx):
+                            corner_first(dy.back(), dx.back(), m).wait_recv()
+                        when(dx.ok, await_corner)
 
         place = lane_of((by, bx)) % 4
 
@@ -491,7 +517,7 @@
 
         def advance(z, slot, hidden):
             hidden = hidden + ready[1, slot] * (ready[0, slot] - hidden)
-            product[z + 1] = mxu(second_left, stacked_shifts(hidden, part))
+            product[z + 1] = mxu(second_left, right_rows(*stacked_shifts(hidden, part)))
             return hidden
 
         def reach(m, first, count, hidden):
@@ -530,9 +556,9 @@
         for target in range(gz):
             packed[target] = fix[bz * target : bz * target + bz + 4, :]
             packed_rim[target] = border[bz * target : bz * target + bz + 4]
-        for ok, make in late:
-            when(ok, lambda make=make: make().start())
+        late(lambda copy: copy.start())
         own_ref[mine] = packed[me]
+        late(lambda copy: copy.wait_send())
 
     for k in range(ranks):
         def await_own(k=k):
@@ -540,17 +566,17 @@
         pl.when(mine != k)(await_own)
     for dy in steps_y:
         def await_beside(dy=dy):
-            halo_last(-dy, 0).wait_recv()
-        when(exists(dy, 0), await_beside)
+            halo_last(dy.back(), 0).wait_recv()
+        when(dy.ok, await_beside)
     for dx in steps_x:
         def await_rims(dx=dx):
             for k in range(ranks):
-                edge_last(-dx, k, 0).wait_recv()
-        when(exists(0, dx), await_rims)
+                edge_last(dx.back(), k, 0).wait_recv()
+        when(dx.ok, await_rims)
         for dy in steps_y:
             def await_corner(dy=dy, dx=dx):
-                corner_last(-dy, -dx, 0).wait_recv()
-            when(exists(dy, dx), await_corner)
+                corner_last(dy.back(), dx.back(), 0).wait_recv()
+            when(both(dy.ok, dx.ok), await_corner)
     place = lane_of((bz + 4, bx)) % 4
     for line in range(by + 4):
         if line < 2:
@@ -562,15 +588,10 @@
         beyond = jnp.where(place < 2, x3[slot, 0], x3[slot, 1])
         edge_ref[line] = pltpu.roll(beyond, (bx - 2 - 4 * j) % bx, 1)
 
-    @pl.when(works)
-    def drain():
-        for ok, make in late:
-            when(ok, lambda make=make: make().wait_send())
-
 
 def segment_kernel(
     sizes, own_ref, beside_ref, edge_ref, in_left_ref, out_left_ref, out_bias_ref,
-    clean_ref, out_ref, shifted, ready, product, result,
+    clean_any, out_any, shifted, ready, product, result, clean, sems,
 ):
     gz, gy, gx = sizes
     ranks = own_ref.shape[0]
@@ -608,14 +629,21 @@
         ready[y] = grown
     for z in range(bz):
         for y in range(by):
-            clean_ref[z, y : y + 1, :] = middle_of(2 + y)[2 + z : 3 + z]
+            clean[z, y : y + 1, :] = middle_of(2 + y)[2 + z : 3 + z]
+    first = pltpu.make_async_copy(clean, clean_any, sems.at[0])
+    first.start()
     for y in range(by + 2):
-        product[y] = mxu(out_left, stacked_shifts(ready[y], bz))
+        high, low = stacked_shifts(ready[y], bz)
+        double = mxu(out_left, high)
+        product[y] = double[0:48] + double[48:96] + mxu(out_left[0:48], low)
         if y >= 2:
             total = product[y - 2, 0:16] + product[y - 1, 16:32] + product[y, 32:48] + out_bias
             for z in range(bz):
                 result[pl.ds(z * by + y - 2, 16, stride=bz * by), :] = total[:, z * bx : (z + 1) * bx]
-    out_ref[...] = result[0 : 16 * bz * by, :]
+    second = pltpu.make_async_copy(result.at[0 : 16 * bz * by, :], out_any, sems.at[1])
+    second.start()
+    first.wait()
+    second.wait()
 
 
 def body(sizes, noisy, first_weight, first_bias, second_weight, second_bias, head_weight,
@@ -655,7 +683,7 @@
             room(2, bz + 4, 2 * bx),
             room(by + 4, bz + 4, bx),
             pltpu.VMEM((16 * (bz + 2), 30 * (bz + 4)), BF16),
-            pltpu.VMEM((48, 432), BF16),
+            pltpu.VMEM((96, 144), BF16),
             room(16, LANES),
         ],
         in_specs=[rest] * len(args),
@@ -697,12 +725,14 @@
             jax.ShapeDtypeStruct((16 * bz * by, bx), F32),
         ],
         in_specs=[vmem] * 6,
-        out_specs=[vmem] * 2,
+        out_specs=[rest] * 2,
         scratch_shapes=[
             room(6, (by + 4) * (bz + 4), bx),
             room(by + 2, 16 * (bz + 2), 2 * bx),
             room(by + 2, 48, bz * bx),
             room(17 * bz * by, bx),
+            room(bz, by, bx),
+            dma((2,)),
         ],
         compiler_params=pltpu.CompilerParams(vmem_limit_bytes=GRANT),
         name="segment",

time: 16.9 us -> 16.6 us (0.982)
  Pallas kernels: 16 us -> 15.7 us
    pallas_call x1, Pallas kernels: 2.03 us -> 1.74 us  [body(): pl.pallas_call(functools.partial(segment_kernel, sizes), out_shape=[jax.S...]
where the time goes in v6:
time: 16.6 us; the launch traced here: 16.3 us
  Pallas kernels  15.7 us (95%)
  between operations  0.64 us (4%)
    pallas_call x1, Pallas kernels, body(): pl.pallas_call(functools.partial(layers_kernel, sizes, ranks, bz, by, bx)...  14 us
    pallas_call x1, Pallas kernels, body(): pl.pallas_call(functools.partial(segment_kernel, sizes), out_shape=[jax.S...  1.74 us

profile of v6, /device:TPU:0, one launch (start us, length us, event | category | flops | bytes accessed | tf_op | source)
XLA Modules:
  0.0 16.3 jit_solution(2659431245618747065)
XLA Ops:
  0.6 14.0 %layers.1 = (f32[2,8,512]{2,1,0:T(8,128)S(1)}, f32[2,8,256]{2,1,0:T(8,128)S(1)}, f32[12,8,128]{2,1,0:T(8,128)S(1)}, bf16[96,240]{1,0:T(8,128)(2,1)S(1)}, bf16[96...) custom-call(f32[32,128]{1,0:T(8,128)} %bitcast.10, f32[27,1,32]{2,1,0:T(1,128)} %bitcast.11, f32[1,16]{1,0:T(1,128)} %bitcast.12, ...), custom_call_target="tpu_custom_call" | custom-call | tf_op jit(solution)/shard_map/layers/pallas_call | solution.py:679
  14.6 1.7 %segment.1 = (f32[4,8,128]{2,1,0:T(8,128)}, f32[512,128]{1,0:T(8,128)}) custom-call(f32[2,8,512]{2,1,0:T(8,128)S(1)} %get-tuple-element.10.own_ref, f32[2,8,256]{2,1,0:T(8,128)S(1)} %get-tuple-element.11.beside_ref, f32[12,8,128]{2,1,0:T(8,128)S(1)} %get-tuple-element.12.edge_ref, bf16[96,240]{1,0:T(8,128)(2,1)S(1)} %get-tuple-element.13.in_left_ref, ...), custom_call_target="tpu_custom_call" | custom-call | tf_op jit(solution)/shard_map/segment/pallas_call | solution.py:721

commit v7 on v6

--- a/solution.py
+++ b/solution.py
@@ -8,7 +8,7 @@
 from jax.sharding import PartitionSpec as P
 
 LANES = 128
-GRANT = 40 << 20
+GRANT = 48 << 20
 F32 = jnp.float32
 BF16 = jnp.bfloat16
 MESH = pl.DeviceIdType.MESH
@@ -195,7 +195,7 @@
     own_ref, beside_ref, edge_ref, in_left_ref, out_left_ref, out_bias_ref,
     noisy_ref, w1_ref, b1_ref, w2_ref, b2_ref, head_ref, w3_ref, b3_ref, w4_ref, b4_ref, load_sem,
     m1, my, x1, halo, rim, send1, recv1,
-    shifted, ready, product, fix, packed, packed_rim,
+    shifted, ready, product, settled, fix, packed, packed_rim,
     x3, own_send, own_recv, beside_send, beside_recv, edge_send, corner_send, edge_recv,
 ):
     gz, gy, gx = sizes
@@ -415,7 +415,7 @@
             device_id_type=MESH,
         )
 
-    def late(act):
+    def late(act, pack=lambda targets: None):
         def to_beside(dy, targets):
             for target in targets:
                 act(halo_last(dy, target))
@@ -429,12 +429,14 @@
             for dx in steps_x:
                 when(dx.ok, lambda: act(edge_last(dx, mine, target)))
 
+        pack(range(ranks))
         for dy in steps_y:
             when(beside(dy), functools.partial(to_beside, dy, range(ranks)))
         for k in range(1, ranks):
             to_own(lax.rem(me + k, ranks))
         for target in range(ranks):
             to_edge(target)
+        pack(range(ranks, gz))
         for target in range(ranks, gz):
             to_own(target)
             to_edge(target)
@@ -520,27 +522,32 @@
             product[z + 1] = mxu(second_left, right_rows(*stacked_shifts(hidden, part)))
             return hidden
 
-        def reach(m, first, count, hidden):
+        def settle(z):
+            pre = product[z, 0:32] + product[z + 1, 32:64] + product[z + 2, 64:96]
+            settled[0, z] = jnp.tanh(pre[0:16])
+            settled[1, z] = jax.nn.sigmoid(pre[16:32] + second_bias)
+
+        def reach(m, first, count, hidden, start=0):
             arrive(m)
             gather(m)
             for slot in range(count):
                 gates(first + slot, slot)
             for slot in range(count):
                 hidden = advance(first + slot, slot, hidden)
+                if slot >= start:
+                    settle(first + slot - 1)
             return hidden
 
         def later(i, hidden):
             return reach(i + 1, (i + 1) * bz - 1, bz, hidden)
 
-        hidden = reach(0, 0, bz - 1, jnp.zeros((16 * rows, 2 * bx), F32))
+        hidden = reach(0, 0, bz - 1, jnp.zeros((16 * rows, 2 * bx), F32), 1)
         hidden = times(gz - 2, later, hidden)
         reach(gz - 1, depth - bz - 1, bz + 1, hidden)
+        settle(depth - 1)
 
         def back(z, hidden):
-            pre = product[z, 0:32] + product[z + 1, 32:64] + product[z + 2, 64:96]
-            cand = jnp.tanh(pre[0:16])
-            change = jax.nn.sigmoid(pre[16:32] + second_bias)
-            hidden = hidden + change * (cand - hidden)
+            hidden = hidden + settled[1, z] * (settled[0, z] - hidden)
             fix[pl.ds(z + 2, 1), :] = jnp.sum(head * hidden, axis=0, keepdims=True)
             return hidden
 
@@ -553,10 +560,12 @@
             fix[2 : 2 + depth, lanes] = fix[2 : 2 + depth, lanes] + centre
             turned = pltpu.roll(fix[:, lanes], 4 * j + 2, 1)
             border = jnp.where((lane >= 4 * j) & (lane < 4 * j + 4), turned, border)
-        for target in range(gz):
-            packed[target] = fix[bz * target : bz * target + bz + 4, :]
-            packed_rim[target] = border[bz * target : bz * target + bz + 4]
-        late(lambda copy: copy.start())
+        def pack(targets):
+            for target in targets:
+                packed[target] = fix[bz * target : bz * target + bz + 4, :]
+                packed_rim[target] = border[bz * target : bz * target + bz + 4]
+
+        late(lambda copy: copy.start(), pack)
         own_ref[mine] = packed[me]
         late(lambda copy: copy.wait_send())
 
@@ -701,6 +710,7 @@
             room(6, (depth + 2) * lines, bx),
             room(2, bz + 1, 16 * (part + 2), 2 * bx),
             room(depth + 2, 96, part * bx),
+            room(2, depth, 16, part * bx),
             room(depth + 16, part * bx),
             room(gz, bz + 4, part * bx),
             room(gz, bz + 4, bx),

time: 16.6 us -> 16.6 us (level)
  no operation moved by 1% of the time
where the time goes in v7:
time: 16.6 us; the launch traced here: 16.3 us
  Pallas kernels  15.7 us (95%)
  between operations  0.64 us (4%)
    pallas_call x1, Pallas kernels, body(): pl.pallas_call(functools.partial(layers_kernel, sizes, ranks, bz, by, bx)...  13.9 us
    pallas_call x1, Pallas kernels, body(): pl.pallas_call(functools.partial(segment_kernel, sizes), out_shape=[jax.S...  1.75 us

profile of v7, /device:TPU:0, one launch (start us, length us, event | category | flops | bytes accessed | tf_op | source)
XLA Modules:
  0.0 16.3 jit_solution(14359412680767335175)
XLA Ops:
  0.6 13.9 %layers.1 = (f32[2,8,512]{2,1,0:T(8,128)S(1)}, f32[2,8,256]{2,1,0:T(8,128)S(1)}, f32[12,8,128]{2,1,0:T(8,128)S(1)}, bf16[96,240]{1,0:T(8,128)(2,1)S(1)}, bf16[96...) custom-call(f32[32,128]{1,0:T(8,128)} %bitcast.10, f32[27,1,32]{2,1,0:T(1,128)} %bitcast.11, f32[1,16]{1,0:T(1,128)} %bitcast.12, ...), custom_call_target="tpu_custom_call" | custom-call | tf_op jit(solution)/shard_map/layers/pallas_call | solution.py:688
  14.6 1.7 %segment.1 = (f32[4,8,128]{2,1,0:T(8,128)}, f32[512,128]{1,0:T(8,128)}) custom-call(f32[2,8,512]{2,1,0:T(8,128)S(1)} %get-tuple-element.10.own_ref, f32[2,8,256]{2,1,0:T(8,128)S(1)} %get-tuple-element.11.beside_ref, f32[12,8,128]{2,1,0:T(8,128)S(1)} %get-tuple-element.12.edge_ref, bf16[96,240]{1,0:T(8,128)(2,1)S(1)} %get-tuple-element.13.in_left_ref, ...), custom_call_target="tpu_custom_call" | custom-call | tf_op jit(solution)/shard_map/segment/pallas_call | solution.py:731

commit v8 on v7

--- a/solution.py
+++ b/solution.py
@@ -641,15 +641,20 @@
             clean[z, y : y + 1, :] = middle_of(2 + y)[2 + z : 3 + z]
     first = pltpu.make_async_copy(clean, clean_any, sems.at[0])
     first.start()
+    totals = []
     for y in range(by + 2):
         high, low = stacked_shifts(ready[y], bz)
         double = mxu(out_left, high)
         product[y] = double[0:48] + double[48:96] + mxu(out_left[0:48], low)
         if y >= 2:
-            total = product[y - 2, 0:16] + product[y - 1, 16:32] + product[y, 32:48] + out_bias
-            for z in range(bz):
-                result[pl.ds(z * by + y - 2, 16, stride=bz * by), :] = total[:, z * bx : (z + 1) * bx]
-    second = pltpu.make_async_copy(result.at[0 : 16 * bz * by, :], out_any, sems.at[1])
+            totals.append(product[y - 2, 0:16] + product[y - 1, 16:32] + product[y, 32:48] + out_bias)
+    for z in range(bz):
+        stack = jnp.stack([total[:, z * bx : (z + 1) * bx] for total in totals], axis=0)
+        turned = jnp.transpose(stack, (1, 0, 2))
+        for o in range(16):
+            row = (o * bz + z) * by
+            result[row : row + by, :] = turned[o]
+    second = pltpu.make_async_copy(result, out_any, sems.at[1])
     second.start()
     first.wait()
     second.wait()
@@ -740,7 +745,7 @@
             room(6, (by + 4) * (bz + 4), bx),
             room(by + 2, 16 * (bz + 2), 2 * bx),
             room(by + 2, 48, bz * bx),
-            room(17 * bz * by, bx),
+            room(16 * bz * by, bx),
             room(bz, by, bx),
             dma((2,)),
         ],

time: 16.6 us -> 16.5 us (level)
  no operation moved by 1% of the time
where the time goes in v8:
time: 16.5 us; the launch traced here: 16.3 us
  Pallas kernels  15.6 us (95%)
  between operations  0.64 us (4%)
    pallas_call x1, Pallas kernels, body(): pl.pallas_call(functools.partial(layers_kernel, sizes, ranks, bz, by, bx)...  13.9 us
    pallas_call x1, Pallas kernels, body(): pl.pallas_call(functools.partial(segment_kernel, sizes), out_shape=[jax.S...  1.72 us

profile of v8, /device:TPU:0, one launch (start us, length us, event | category | flops | bytes accessed | tf_op | source)
XLA Modules:
  0.0 16.3 jit_solution(2943271429573965996)
XLA Ops:
  0.6 13.9 %layers.1 = (f32[2,8,512]{2,1,0:T(8,128)S(1)}, f32[2,8,256]{2,1,0:T(8,128)S(1)}, f32[12,8,128]{2,1,0:T(8,128)S(1)}, bf16[96,240]{1,0:T(8,128)(2,1)S(1)}, bf16[96...) custom-call(f32[32,128]{1,0:T(8,128)} %bitcast.10, f32[27,1,32]{2,1,0:T(1,128)} %bitcast.11, f32[1,16]{1,0:T(1,128)} %bitcast.12, ...), custom_call_target="tpu_custom_call" | custom-call | tf_op jit(solution)/shard_map/layers/pallas_call | solution.py:693
  14.6 1.7 %segment.1 = (f32[4,8,128]{2,1,0:T(8,128)}, f32[512,128]{1,0:T(8,128)}) custom-call(f32[2,8,512]{2,1,0:T(8,128)S(1)} %get-tuple-element.10.own_ref, f32[2,8,256]{2,1,0:T(8,128)S(1)} %get-tuple-element.11.beside_ref, f32[12,8,128]{2,1,0:T(8,128)S(1)} %get-tuple-element.12.edge_ref, bf16[96,240]{1,0:T(8,128)(2,1)S(1)} %get-tuple-element.13.in_left_ref, ...), custom_call_target="tpu_custom_call" | custom-call | tf_op jit(solution)/shard_map/segment/pallas_call | solution.py:736

commit v9 on v7

--- a/solution.py
+++ b/solution.py
@@ -517,10 +517,13 @@
             ready[0, slot] = mask * jnp.tanh(pre[0 : 16 * rows])
             ready[1, slot] = jax.nn.sigmoid(pre[16 * rows :])
 
-        def advance(z, slot, hidden):
+        def advance(slot, hidden):
             hidden = hidden + ready[1, slot] * (ready[0, slot] - hidden)
-            product[z + 1] = mxu(second_left, right_rows(*stacked_shifts(hidden, part)))
+            ready[0, slot] = hidden
             return hidden
+
+        def spread(z, slot):
+            product[z + 1] = mxu(second_left, right_rows(*stacked_shifts(ready[0, slot], part)))
 
         def settle(z):
             pre = product[z, 0:32] + product[z + 1, 32:64] + product[z + 2, 64:96]
@@ -533,7 +536,9 @@
             for slot in range(count):
                 gates(first + slot, slot)
             for slot in range(count):
-                hidden = advance(first + slot, slot, hidden)
+                hidden = advance(slot, hidden)
+            for slot in range(count):
+                spread(first + slot, slot)
                 if slot >= start:
                     settle(first + slot - 1)
             return hidden

time: 16.6 us -> 16.6 us (level)
  no operation moved by 1% of the time
where the time goes in v9:
time: 16.6 us; the launch traced here: 16.3 us
  Pallas kernels  15.7 us (95%)
  between operations  0.64 us (4%)
    pallas_call x1, Pallas kernels, body(): pl.pallas_call(functools.partial(layers_kernel, sizes, ranks, bz, by, bx)...  13.9 us
    pallas_call x1, Pallas kernels, body(): pl.pallas_call(functools.partial(segment_kernel, sizes), out_shape=[jax.S...  1.74 us

profile of v9, /device:TPU:0, one launch (start us, length us, event | category | flops | bytes accessed | tf_op | source)
XLA Modules:
  0.0 16.3 jit_solution(2183409004832893316)
XLA Ops:
  0.6 13.9 %layers.1 = (f32[2,8,512]{2,1,0:T(8,128)S(1)}, f32[2,8,256]{2,1,0:T(8,128)S(1)}, f32[12,8,128]{2,1,0:T(8,128)S(1)}, bf16[96,240]{1,0:T(8,128)(2,1)S(1)}, bf16[96...) custom-call(f32[32,128]{1,0:T(8,128)} %bitcast.10, f32[27,1,32]{2,1,0:T(1,128)} %bitcast.11, f32[1,16]{1,0:T(1,128)} %bitcast.12, ...), custom_call_target="tpu_custom_call" | custom-call | tf_op jit(solution)/shard_map/layers/pallas_call | solution.py:693
  14.6 1.7 %segment.1 = (f32[4,8,128]{2,1,0:T(8,128)}, f32[512,128]{1,0:T(8,128)}) custom-call(f32[2,8,512]{2,1,0:T(8,128)S(1)} %get-tuple-element.10.own_ref, f32[2,8,256]{2,1,0:T(8,128)S(1)} %get-tuple-element.11.beside_ref, f32[12,8,128]{2,1,0:T(8,128)S(1)} %get-tuple-element.12.edge_ref, bf16[96,240]{1,0:T(8,128)(2,1)S(1)} %get-tuple-element.13.in_left_ref, ...), custom_call_target="tpu_custom_call" | custom-call | tf_op jit(solution)/shard_map/segment/pallas_call | solution.py:736
